TPU v7x, 512 devices: a whole 4x8x8 slice. The times are simulated.
512 devices in a mesh: docs: 128 (over y, z, core), split: 4 (over x).
Axes of the slice: x: 4, y: 8, z: 8, core: 2. Of those that a mesh axis runs over, the one named last changes fastest.
Arguments:
- embeddings: bfloat16 [65536, 1024], P(('docs', 'split')), may hold values from -480 to 480
- cluster_id: int32 [65536], P(('docs', 'split')), may hold values from 0 to 255, as said below
- rank: int32 [65536], P(('docs', 'split')), may hold values from 0 to 65535, each once
Outputs:
- dup_score: float32 [65536], P(('docs', 'split'))
Inputs may be any that keep to these rules, and one draw needn't show every extreme that they name: `cluster_id`: cluster c belongs to owner c // 2. In each aligned block of 128 documents (the documents of one device) at most 2 documents belong to any one owner, and one owner receives exactly 2 from every block.
All inputs are finite; a program needn't handle non-finite values.
Results may differ from a plain program's by a relative error of at most 0.00056.
Values may be sent and summed in bfloat16 or wider, within the bound.
No kernel may reach another device: no remote copies, remote signals or barrier semaphores. Data moves between devices by JAX's collectives and lax.ppermute only.
A program may use at most 64 MiB of HBM per device.

v0:
```python
import jax
import jax.numpy as jnp
from jax import lax
from jax.sharding import PartitionSpec as P

D = 1024
CL_DEV = 2


EPSILON = 1e-06


def per_device(embeddings, cluster_id, rank):
    values = embeddings.astype(jnp.float32)
    unit = (values / jnp.sqrt(jnp.sum(values * values, axis=1, keepdims=True) + EPSILON)).astype(
        jnp.bfloat16
    )
    owners = lax.axis_size("docs")
    local_docs = embeddings.shape[0]
    capacity = 2 * local_docs // owners
    slots_all = owners * capacity
    owner = cluster_id // CL_DEV
    onehot = (owner[:, None] == jnp.arange(owners, dtype=jnp.int32)[None, :]).astype(jnp.int32)
    before = jnp.cumsum(onehot, axis=0) - onehot
    slot_index = jnp.sum(before * onehot, axis=1)
    target = owner * capacity + slot_index
    send_rows = jnp.zeros((slots_all, D), jnp.bfloat16).at[target].set(unit)
    send_cluster = jnp.full((slots_all,), -1, jnp.int32).at[target].set(cluster_id)
    send_rank = jnp.zeros((slots_all,), jnp.int32).at[target].set(rank)
    got_rows, got_cluster, got_rank = (
        lax.all_to_all(
            send_rows.reshape(owners, capacity, D), "docs", split_axis=0, concat_axis=0, tiled=True
        ),
        lax.all_to_all(
            send_cluster.reshape(owners, capacity), "docs", split_axis=0, concat_axis=0, tiled=True
        ),
        lax.all_to_all(
            send_rank.reshape(owners, capacity), "docs", split_axis=0, concat_axis=0, tiled=True
        ),
    )
    queries = got_rows.reshape(slots_all, D)
    query_cluster = got_cluster.reshape(slots_all)
    query_rank = got_rank.reshape(slots_all)

    def pair_scores(rows_other):
        return jnp.einsum("qd,kd->qk", queries, rows_other, preferred_element_type=jnp.float32)

    def row_best(rows_other, cluster_other, rank_other):
        scores = pair_scores(rows_other)
        allowed = (query_cluster[:, None] == cluster_other[None, :]) & (
            rank_other[None, :] < query_rank[:, None]
        )
        return jnp.max(jnp.where(allowed, scores, -1.0), axis=1)

    start_best = jnp.full((slots_all,), -1.0, jnp.float32)
    rows_piece = lax.all_gather(queries, "split", axis=0, tiled=True)
    cluster_piece = lax.all_gather(query_cluster, "split", axis=0, tiled=True)
    rank_piece = lax.all_gather(query_rank, "split", axis=0, tiled=True)
    total = rows_piece.shape[0]
    pieces = total // slots_all
    stacked = (
        rows_piece.reshape(pieces, slots_all, D),
        cluster_piece.reshape(pieces, slots_all),
        rank_piece.reshape(pieces, slots_all),
    )

    def advance(top_score, member):
        return (jnp.maximum(top_score, row_best(member[0], member[1], member[2])), None)

    result, _ = lax.scan(advance, start_best, stacked)
    top_score = result
    returned_scores = lax.all_to_all(
        top_score.reshape(owners, capacity), "docs", split_axis=0, concat_axis=0, tiled=True
    )
    return returned_scores.reshape(slots_all)[target]


def solution(mesh):
    placed = (P(("docs", "split"), None), P(("docs", "split")), P(("docs", "split")))
    return jax.shard_map(
        per_device, mesh=mesh, in_specs=placed, out_specs=P(("docs", "split")), check_vma=False
    )
```

profile of v0, /device:TPU:1, one launch (start us, length us, event | category | flops | bytes accessed | tf_op | source)
XLA Modules:
  0.0 138.9 jit_solution(11490728331037051452)
XLA Ops:
  8.3 1.1 fusion.5
  9.4 1.8 %scatter_custom_fusion.2 = bf16[256,1024]{1,0:T(8,128)(2,1)S(1)} fusion(s32[128]{0:T(128)S(1)} %compare_select_fusion, bf16[128,1024]{1,0:T(8,128)(2,1)} %param.5, f32[128]{0:T(128)S(1)} %add_sqrt_fusion, bf16[]{:T(256)} %constant.41.clone.1), kind=kCustom, calls=%fused_computation.17 | custom fusion | flops 393216 | bytes 786946 | tf_op jit(solution)/shard_map/scatter | solution.py:27
  11.4 37.6 %all_to_all.38 = bf16[128,2,1024]{2,1,0:T(2,128)(2,1)S(1)} all-to-all(bf16[128,2,1024]{2,1,0:T(2,128)(2,1)S(1)} %reshape.52), channel_id=1, replica_groups=mesh['docs'=128,'split'=4] {'docs'}, dimensions={0} | all-to-all | bytes 1048576 | tf_op jit(solution)/shard_map/all_to_all | solution.py:31
  49.1 1.0 reshape.53
  50.1 1.1 scatter_custom_fusion.1
  51.9 7.2 %all-to-all-start.1 = ((s32[128,1,2]{2,1,0:T(1,128)}), s32[128,1,2]{2,1,0:T(1,128)S(1)}, u32[]{:S(2)}, u32[]{:S(2)}) async-start(s32[128,1,2]{2,1,0:T(1,128)} %bitcast.2), calls=%async_computation.1 | async-start | bytes 131072 | tf_op jit(solution)/shard_map/all_to_all | solution.py:37
  59.1 1.1 scatter_custom_fusion
  61.0 9.8 %all-to-all-done.1 = s32[128,1,2]{2,1,0:T(1,128)S(1)} async-done(((s32[128,1,2]{2,1,0:T(1,128)}), s32[128,1,2]{2,1,0:T(1,128)S(1)}, u32[]{:S(2)}, u32[]{:S(2)}) %all-to-all-start.1) | async-done | bytes 1056 | tf_op jit(solution)/shard_map/all_to_all | solution.py:37
  70.8 5.7 %all-to-all-start = ((s32[128,1,2]{2,1,0:T(1,128)}), s32[128,1,2]{2,1,0:T(1,128)S(1)}, u32[]{:S(2)}, u32[]{:S(2)}) async-start(s32[128,1,2]{2,1,0:T(1,128)} %bitcast), calls=%async_computation | async-start | bytes 131072 | tf_op jit(solution)/shard_map/all_to_all | solution.py:34
  77.1 0.8 reduce.10
  78.1 7.7 %all-gather.1 = s32[4,1,256]{2,1,0:T(1,128)S(1)} all-gather(s32[1,1,256]{2,1,0:T(1,128)S(1)} %reshape.94), channel_id=1, replica_groups=mesh['docs'=128,'split'=4] {'split'}, dimensions={0}, use_global_device_ids=true | all-gather | bytes 5120 | tf_op jit(solution)/shard_map/all_gather | solution.py:58
  85.8 2.4 %all-to-all-done = s32[128,1,2]{2,1,0:T(1,128)S(1)} async-done(((s32[128,1,2]{2,1,0:T(1,128)}), s32[128,1,2]{2,1,0:T(1,128)S(1)}, u32[]{:S(2)}, u32[]{:S(2)}) %all-to-all-start) | async-done | bytes 1056 | tf_op jit(solution)/shard_map/all_to_all | solution.py:34
  88.2 0.8 reduce.9
  89.2 7.7 %all-gather = s32[4,1,256]{2,1,0:T(1,128)S(1)} all-gather(s32[1,1,256]{2,1,0:T(1,128)S(1)} %reshape.92), channel_id=1, replica_groups=mesh['docs'=128,'split'=4] {'split'}, dimensions={0}, use_global_device_ids=true | all-gather | bytes 5120 | tf_op jit(solution)/shard_map/all_gather | solution.py:57
  97.3 6.5 %while.12 = (s32[]{:T(128)}, f32[256]{0:T(256)S(1)}, s32[128,2]{1,0:T(8,128)}, s32[4,256]{1,0:T(4,128)S(1)}, s32[4,256]{1,0:T(4,128)S(1)}, /*index=5*/s32[128,2]...) while((s32[]{:T(128)}, f32[256]{0:T(256)S(1)}, ...), condition=%wide.wide.region_8.9_spmd.clone, body=%wide.wide.region_6.8_spmd.clone.sunk | while | flops 134545664 | bytes 1061507 | solution.py:70
  97.3 1.6 %fusion.25 = f32[256]{0:T(256)S(1)} fusion(bf16[256,1024]{1,0:T(8,128)(2,1)} %get-tuple-element.222, bf16[4,256,1024]{2,1,0:T(8,128)(2,1)} %get-tuple-element.221, s32[]{:T(128)} %get-tuple-element.203, s32[256]{0:T(256)S(1)} %get-tuple-element.223, s32[256]{0:T(256)S(1)} %get-tuple-element.224, s32[256]{0:T(256)S(1)} %bitcast.43, ...), kind=kOutput, calls=%fused_computation.6.clone.clone.1 | convolution fusion | flops 134545152 | bytes 1054208 | tf_op jit(solution)/shard_map/while/body/eval_jaxpr/qd,kd->qk/dot_general | solution.py:46
  98.9 1.6 %fusion.25 = f32[256]{0:T(256)S(1)} fusion(bf16[256,1024]{1,0:T(8,128)(2,1)} %get-tuple-element.222, bf16[4,256,1024]{2,1,0:T(8,128)(2,1)} %get-tuple-element.221, s32[]{:T(128)} %get-tuple-element.203, s32[256]{0:T(256)S(1)} %get-tuple-element.223, s32[256]{0:T(256)S(1)} %get-tuple-element.224, s32[256]{0:T(256)S(1)} %bitcast.43, ...), kind=kOutput, calls=%fused_computation.6.clone.clone.1 | convolution fusion | flops 134545152 | bytes 1054208 | tf_op jit(solution)/shard_map/while/body/eval_jaxpr/qd,kd->qk/dot_general | solution.py:46
  100.5 1.6 %fusion.25 = f32[256]{0:T(256)S(1)} fusion(bf16[256,1024]{1,0:T(8,128)(2,1)} %get-tuple-element.222, bf16[4,256,1024]{2,1,0:T(8,128)(2,1)} %get-tuple-element.221, s32[]{:T(128)} %get-tuple-element.203, s32[256]{0:T(256)S(1)} %get-tuple-element.223, s32[256]{0:T(256)S(1)} %get-tuple-element.224, s32[256]{0:T(256)S(1)} %bitcast.43, ...), kind=kOutput, calls=%fused_computation.6.clone.clone.1 | convolution fusion | flops 134545152 | bytes 1054208 | tf_op jit(solution)/shard_map/while/body/eval_jaxpr/qd,kd->qk/dot_general | solution.py:46
  102.1 1.6 %fusion.25 = f32[256]{0:T(256)S(1)} fusion(bf16[256,1024]{1,0:T(8,128)(2,1)} %get-tuple-element.222, bf16[4,256,1024]{2,1,0:T(8,128)(2,1)} %get-tuple-element.221, s32[]{:T(128)} %get-tuple-element.203, s32[256]{0:T(256)S(1)} %get-tuple-element.223, s32[256]{0:T(256)S(1)} %get-tuple-element.224, s32[256]{0:T(256)S(1)} %bitcast.43, ...), kind=kOutput, calls=%fused_computation.6.clone.clone.1 | convolution fusion | flops 134545152 | bytes 1054208 | tf_op jit(solution)/shard_map/while/body/eval_jaxpr/qd,kd->qk/dot_general | solution.py:46
  103.7 0.8 all_to_all.32
  104.5 12.7 %all-to-all-start.3 = ((f32[128,1,2]{2,1,0:T(1,128)}), f32[128,1,2]{2,1,0:T(1,128)S(1)}, u32[]{:S(2)}, u32[]{:S(2)}) async-start(f32[128,1,2]{2,1,0:T(1,128)} %bitcast.5), calls=%async_computation.3 | async-start | bytes 131072 | tf_op jit(solution)/shard_map/all_to_all | solution.py:72
  117.2 11.6 %all-to-all-done.3 = f32[128,1,2]{2,1,0:T(1,128)S(1)} async-done(((f32[128,1,2]{2,1,0:T(1,128)}), f32[128,1,2]{2,1,0:T(1,128)S(1)}, u32[]{:S(2)}, u32[]{:S(2)}) %all-to-all-start.3) | async-done | bytes 1056 | tf_op jit(solution)/shard_map/all_to_all | solution.py:72
  129.3 0.8 reduce.11
  130.3 1.8 %gather_fusion = f32[128]{0:T(128)} fusion(f32[256]{0:T(256)S(1)} %reshape.55, s32[1024]{0:T(1024)S(1)} %pad_clamp_fusion), kind=kCustom, calls=%fused_computation | custom fusion | bytes 1536 | tf_op jit(solution)/shard_map/gather | solution.py:75
  (35 shorter events, 5.4 us)
Async XLA Ops:
  6.5 90.7 %all-gather.4.cloned.1.call-start = ((), (), s32[]{:S(2)}) async-start(), calls=%async_computation.4 | async-start | bytes 2621440 | tf_op jit(solution)/shard_map/all_gather | solution.py:56
  51.9 18.9 %all-to-all-start.1 = ((s32[128,1,2]{2,1,0:T(1,128)}), s32[128,1,2]{2,1,0:T(1,128)S(1)}, u32[]{:S(2)}, u32[]{:S(2)}) async-start(s32[128,1,2]{2,1,0:T(1,128)} %bitcast.2), calls=%async_computation.1 | async-start | bytes 131072 | tf_op jit(solution)/shard_map/all_to_all | solution.py:37
  70.8 26.4 %copy-start = (s32[128,1,2]{2,1,0:T(1,128)}, s32[128,1,2]{2,1,0:T(1,128)S(1)}, u32[]{:S(2)}) copy-start(s32[128,1,2]{2,1,0:T(1,128)S(1)} %all-to-all-done.1) | copy-start | bytes 3076
  70.8 17.4 %all-to-all-start = ((s32[128,1,2]{2,1,0:T(1,128)}), s32[128,1,2]{2,1,0:T(1,128)S(1)}, u32[]{:S(2)}, u32[]{:S(2)}) async-start(s32[128,1,2]{2,1,0:T(1,128)} %bitcast), calls=%async_computation | async-start | bytes 131072 | tf_op jit(solution)/shard_map/all_to_all | solution.py:34
  88.2 9.0 %copy-start.1 = (s32[128,1,2]{2,1,0:T(1,128)}, s32[128,1,2]{2,1,0:T(1,128)S(1)}, u32[]{:S(2)}) copy-start(s32[128,1,2]{2,1,0:T(1,128)S(1)} %all-to-all-done) | copy-start | bytes 3076
  104.5 24.3 %all-to-all-start.3 = ((f32[128,1,2]{2,1,0:T(1,128)}), f32[128,1,2]{2,1,0:T(1,128)S(1)}, u32[]{:S(2)}, u32[]{:S(2)}) async-start(f32[128,1,2]{2,1,0:T(1,128)} %bitcast.5), calls=%async_computation.3 | async-start | bytes 131072 | tf_op jit(solution)/shard_map/all_to_all | solution.py:72
Sparse Core Ops, SparseCore 0:
  50.2 29.5 all-gather.3
where the time goes:
time: 139 us
  blocking collectives  53.1 us (38%)
  starting transfers between devices  25.6 us (18%)
  waiting for transfers between devices  23.8 us (17%)
  between operations  13.5 us (10%)
  local copies, waits for them, and re-layouts  9.27 us (7%)
  other arithmetic  7.19 us (5%)
  matrix products  6.24 us (4%)
    all_to_all x1, blocking collectives, per_device(): lax.all_to_all(send_rows.reshape(owners, capacity, D), 'docs', split_axis...  37.6 us
    all_to_all x1, starting transfers between devices, per_device(): lax.all_to_all(top_score.reshape(owners, capacity), 'docs', split_axis=0,...  12.7 us
    all_to_all x1, waiting for transfers between devices, per_device(): lax.all_to_all(top_score.reshape(owners, capacity), 'docs', split_axis=0,...  11.6 us
    all_to_all x1, waiting for transfers between devices, per_device(): lax.all_to_all(send_rank.reshape(owners, capacity), 'docs', split_axis=0,...  9.83 us
    all_gather x1, blocking collectives, per_device(): cluster_piece = lax.all_gather(query_cluster, 'split', axis=0, tiled=True)  7.72 us
    all_gather x1, blocking collectives, per_device(): rank_piece = lax.all_gather(query_rank, 'split', axis=0, tiled=True)  7.71 us
    all_to_all x1, starting transfers between devices, per_device(): lax.all_to_all(send_rank.reshape(owners, capacity), 'docs', split_axis=0,...  7.17 us
    dot_general x4, matrix products, pair_scores(): jnp.einsum('qd,kd->qk', queries, rows_other, preferred_element_type=jnp.f...  6.24 us
  transfers between devices with their start and end apart: 4, of which 3 were waited for; matrix products, arithmetic and copies ran while one was open for 4% of the time, Pallas kernels for 0%

commit v1 on v0

v1 whole, which is shorter than its diff:
```python
import jax
import jax.numpy as jnp
from jax import lax
from jax.experimental import pallas as pl
from jax.experimental.pallas import tpu as pltpu
from jax.sharding import PartitionSpec as P

EPSILON = 1e-06
SLOTS = 2
LANES = 128


def pack_kernel(rows_ref, cluster_ref, rank_ref, send_ref, place_ref):
    docs, width = rows_ref.shape
    slots = send_ref.shape[0]
    values = rows_ref[...].astype(jnp.float32)
    total = jnp.sum(values * values, axis=1, keepdims=True)
    unit = (values / jnp.sqrt(total + EPSILON)).astype(jnp.bfloat16)
    cluster = jnp.broadcast_to(cluster_ref[...], (docs, docs))
    rank = jnp.broadcast_to(rank_ref[...], (docs, docs))
    row = lax.broadcasted_iota(jnp.int32, (docs, docs), 0)
    col = lax.broadcasted_iota(jnp.int32, (docs, docs), 1)
    cluster_col = jnp.sum(jnp.where(row == col, cluster, 0), axis=1, keepdims=True)
    rank_col = jnp.sum(jnp.where(row == col, rank, 0), axis=1, keepdims=True)
    earlier = (cluster_col == cluster) & (row < col)
    slot = jnp.sum(earlier.astype(jnp.int32), axis=0, keepdims=True)
    place = cluster_ref[...] * SLOTS + slot
    place_ref[...] = place
    age = 65536 - rank_col
    high = age // 256
    low = age - high * 256
    lane = lax.broadcasted_iota(jnp.int32, (docs, LANES), 1)
    digits = jnp.where(lane == 0, high, jnp.where(lane == 1, low, 0))
    digits = digits.astype(jnp.float32).astype(jnp.bfloat16)
    target = lax.broadcasted_iota(jnp.int32, (slots, docs), 0)
    onehot = (target == jnp.broadcast_to(place, (slots, docs))).astype(jnp.float32).astype(jnp.bfloat16)
    send_ref[:, :width] = jnp.dot(onehot, unit, preferred_element_type=jnp.float32).astype(jnp.bfloat16)
    send_ref[:, width:] = jnp.dot(onehot, digits, preferred_element_type=jnp.float32).astype(jnp.bfloat16)


def ages(rows_ref, width):
    lane = lax.broadcasted_iota(jnp.int32, (LANES, LANES), 0)
    weight = jnp.where(lane == 0, 256.0, jnp.where(lane == 1, 1.0, 0.0)).astype(jnp.bfloat16)
    return weight, rows_ref[:, width:]


def best_of(keys_ref, queries_ref, width):
    weight, key_digits = ages(keys_ref, width)
    key_age = jnp.dot(key_digits, weight, preferred_element_type=jnp.float32)
    lane = lax.broadcasted_iota(jnp.int32, (8, LANES), 1)
    weight_row = jnp.where(lane == 0, 256.0, jnp.where(lane == 1, 1.0, 0.0)).astype(jnp.bfloat16)
    contract = (((1,), (1,)), ((), ()))
    query_age = lax.dot_general(weight_row, queries_ref[:, width:], contract, preferred_element_type=jnp.float32)
    count = queries_ref.shape[0]
    scores = lax.dot_general(keys_ref[:, :width], queries_ref[:, :width], contract, preferred_element_type=jnp.float32)
    allowed = key_age[:, :1] > query_age[:1, :]
    return jnp.max(jnp.where(allowed, scores, -1.0), axis=0, keepdims=True)


def make_own(width):
    def kernel(queries_ref, best_ref):
        best_ref[...] = best_of(queries_ref, queries_ref, width)

    return kernel


def make_peer(width):
    def kernel(queries_ref, keys_ref, best_ref, out_ref):
        best = jnp.maximum(best_ref[...], best_of(keys_ref, queries_ref, width))
        messages = out_ref.shape[0]
        count = best.shape[1]
        best = jnp.broadcast_to(best, (messages, count))
        row = lax.broadcasted_iota(jnp.int32, (messages, count), 0) * SLOTS
        col = lax.broadcasted_iota(jnp.int32, (messages, count), 1)
        first = jnp.sum(jnp.where(col == row, best, 0.0), axis=1, keepdims=True)
        second = jnp.sum(jnp.where(col == row + 1, best, 0.0), axis=1, keepdims=True)
        lane = lax.broadcasted_iota(jnp.int32, out_ref.shape, 1)
        out_ref[...] = jnp.where(lane == 0, first, second)

    return kernel


def unpack_kernel(scores_ref, place_ref, out_ref):
    clusters = scores_ref.shape[0]
    docs = place_ref.shape[1]
    place = jnp.broadcast_to(place_ref[...], (clusters, docs))
    row = lax.broadcasted_iota(jnp.int32, (clusters, docs), 0) * SLOTS
    first = jnp.where(place == row, scores_ref[:, 0:1], 0.0)
    second = jnp.where(place == row + 1, scores_ref[:, 1:2], 0.0)
    out_ref[...] = jnp.sum(first + second, axis=0, keepdims=True)


def make_per_device(docs_axis, split_axis):
    devices = docs_axis * split_axis
    clusters = devices // 2
    slots = clusters * SLOTS

    groups = [
        [d * split_axis + s for d in range(core, docs_axis, 2) for s in range(split_axis)]
        for core in range(2)
    ]
    partner = [(d, d ^ 1) for d in range(docs_axis)]
    both = ("docs", "split")

    def per_device(embeddings, cluster_id, rank):
        docs, width = embeddings.shape
        wide = width + LANES
        send, place = pl.pallas_call(
            pack_kernel,
            out_shape=(
                jax.ShapeDtypeStruct((slots, wide), jnp.bfloat16),
                jax.ShapeDtypeStruct((1, docs), jnp.int32),
            ),
            name="pack",
        )(embeddings, cluster_id.reshape(1, docs), rank.reshape(1, docs))
        got = lax.all_to_all(
            send.reshape(clusters, SLOTS, wide), both, 0, 0, axis_index_groups=groups, tiled=True
        )
        queries = got.reshape(slots, wide)
        keys = lax.ppermute(queries, "docs", partner)
        best = pl.pallas_call(
            make_own(width), out_shape=jax.ShapeDtypeStruct((1, slots), jnp.float32), name="own"
        )(queries)
        scores = pl.pallas_call(
            make_peer(width),
            out_shape=jax.ShapeDtypeStruct((clusters, LANES), jnp.float32),
            name="peer",
        )(queries, keys, best)
        back = lax.all_to_all(
            scores.reshape(clusters, 1, LANES), both, 0, 0, axis_index_groups=groups, tiled=True
        ).reshape(clusters, LANES)
        out = pl.pallas_call(
            unpack_kernel, out_shape=jax.ShapeDtypeStruct((1, docs), jnp.float32), name="unpack"
        )(back, place)
        return out.reshape(docs)

    return per_device


def solution(mesh):
    placed = (P(("docs", "split"), None), P(("docs", "split")), P(("docs", "split")))
    per_device = make_per_device(mesh.shape["docs"], mesh.shape["split"])
    return jax.shard_map(
        per_device, mesh=mesh, in_specs=placed, out_specs=P(("docs", "split")), check_vma=False
    )
```

time: 139 us -> 97 us (0.70)
  blocking collectives: 53.1 us -> 77.1 us
  waiting for transfers between devices: 23.8 us -> 0.01 us
  starting transfers between devices: 25.6 us -> 5.03 us
  between operations: 13.5 us -> 0.04 us
  Pallas kernels: 0 us -> 10.1 us
  other arithmetic: 7.19 us -> 0 us
  matrix products: 6.24 us -> 0 us
  local copies, waits for them, and re-layouts: 9.27 us -> 4.36 us
    all_to_all x1 -> x2, blocking collectives: 37.6 us -> 77.1 us  [the longest x1 54.1 us: per_device(): lax.all_to_all(send.reshape(clusters, SLOTS, wide), both, 0, 0, axis_inde...]
    all_to_all x3 -> x0, starting transfers between devices: 25.6 us -> none  [the longest x1 12.7 us: per_device(): lax.all_to_all(top_score.reshape(owners, capacity), 'docs', split_axis=0,...]
    all_to_all x3 -> x0, waiting for transfers between devices: 23.8 us -> none  [the longest x1 11.6 us: per_device(): lax.all_to_all(top_score.reshape(owners, capacity), 'docs', split_axis=0,...]
    all_gather x2 -> x0, blocking collectives: 15.4 us -> none  [the longest x1 7.72 us: per_device(): cluster_piece = lax.all_gather(query_cluster, 'split', axis=0, tiled=True)]
    pallas_call x0 -> x4, Pallas kernels: none -> 10.1 us  [the longest x1 3.27 us: per_device(): pl.pallas_call(make_peer(width), out_shape=jax.ShapeDtypeStruct((clusters...]
    dot_general x4 -> x0, matrix products: 6.24 us -> none  [pair_scores(): jnp.einsum('qd,kd->qk', queries, rows_other, preferred_element_type=jnp.f...]
    ppermute x0 -> x1, starting transfers between devices: none -> 5.03 us  [per_device(): keys = lax.ppermute(queries, 'docs', partner)]
    all_to_all x5 -> x0, local copies, waits for them, and re-layouts: 3.36 us -> none  [the longest x2 1.33 us: per_device(): lax.all_to_all(send_cluster.reshape(owners, capacity), 'docs', split_axis...]
  transfers between devices with their start and end apart: 4 -> 1, of which waited for: 3 -> 0; matrix products, arithmetic and copies ran while one was open for 4% -> 0% of each run, Pallas kernels for 0% -> 3%
where the time goes in v1:
time: 97 us; the launch traced here: 96.6 us
  blocking collectives  77.1 us (79%)
  Pallas kernels  10.1 us (10%)
  starting transfers between devices  5.03 us (5%)
  local copies, waits for them, and re-layouts  4.36 us (4%)
    all_to_all x1, blocking collectives, per_device(): lax.all_to_all(send.reshape(clusters, SLOTS, wide), both, 0, 0, axis_inde...  54.1 us
    all_to_all x1, blocking collectives, per_device(): lax.all_to_all(scores.reshape(clusters, 1, LANES), both, 0, 0, axis_index...  23 us
    ppermute x1, starting transfers between devices, per_device(): keys = lax.ppermute(queries, 'docs', partner)  5.03 us
    pallas_call x1, Pallas kernels, per_device(): pl.pallas_call(make_peer(width), out_shape=jax.ShapeDtypeStruct((clusters...  3.27 us
    reshape x1, local copies, waits for them, and re-layouts, per_device(): send.reshape(clusters, SLOTS, wide)  2.85 us
    pallas_call x1, Pallas kernels, per_device(): pl.pallas_call(make_own(width), out_shape=jax.ShapeDtypeStruct((1, slots)...  2.64 us
    pallas_call x1, Pallas kernels, per_device(): pl.pallas_call(pack_kernel, out_shape=(jax.ShapeDtypeStruct((slots, wide)...  2.61 us
  transfers between devices with their start and end apart: 1, of which 0 were waited for; matrix products, arithmetic and copies ran while one was open for 0% of the time, Pallas kernels for 3%

profile of v1, /device:TPU:1, one launch (start us, length us, event | category | flops | bytes accessed | tf_op | source)
XLA Modules:
  0.0 96.6 jit_solution(7107396390348655299)
XLA Ops:
  0.0 2.6 %pack.1 = (bf16[512,1152]{1,0:T(8,128)(2,1)}, s32[1,128]{1,0:T(1,128)}) custom-call(bf16[128,1024]{1,0:T(8,128)(2,1)} %rows_ref.1, s32[1,128]{1,0:T(1,128)} %bitcast.9, s32[1,128]{1,0:T(1,128)} %bitcast.10), custom_call_target="tpu_custom_call" | custom-call | tf_op jit(solution)/shard_map/pack/pallas_call | solution.py:108
  2.6 2.9 %reshape.23 = bf16[256,2,1152]{2,1,0:T(2,128)(2,1)S(1)} reshape(bf16[512,1152]{1,0:T(8,128)(2,1)} %get-tuple-element.7) | data formatting | bytes 2359296 | tf_op jit(solution)/shard_map/reshape | solution.py:117
  5.5 54.1 %all_to_all.10 = bf16[256,2,1152]{2,1,0:T(2,128)(2,1)S(1)} all-to-all(bf16[256,2,1152]{2,1,0:T(2,128)(2,1)S(1)} %reshape.23), channel_id=1, replica_groups={{0,1,2,3,8,9,10,11,16,17,18,19,24,25,26,27,32,33,34,35,40,41,42,43,48,4..., dimensions={0} | all-to-all | bytes 2359296 | tf_op jit(solution)/shard_map/all_to_all | solution.py:116
  59.6 0.5 reshape.24.queries_ref
  60.0 0.0 copy-start
  60.1 5.0 %collective-permute-start = (bf16[512,1152]{1,0:T(8,128)(2,1)S(1)}, bf16[512,1152]{1,0:T(8,128)(2,1)S(1)}, u32[]{:S(2)}, u32[]{:S(2)}) collective-permute-start(bf16[512,1152]{1,0:T(8,128)(2,1)S(1)} %reshape.24.queries_ref), channel_id=1, source_target_pairs={{0,4},{4,0},{8,12},{12,8},{16,20},{20,16},{24,28},{28,24},{32,36},... | collective-permute-start | bytes 3538952 | tf_op jit(solution)/shard_map/ppermute | solution.py:120
  65.1 0.0 copy-done
  65.1 2.6 %own.1.best_ref = f32[1,512]{1,0:T(1,128)} custom-call(bf16[512,1152]{1,0:T(8,128)(2,1)} %copy-done), custom_call_target="tpu_custom_call" | custom-call | tf_op jit(solution)/shard_map/own/pallas_call | solution.py:121
  67.7 0.0 collective-permute-done.keys_ref
  67.8 0.0 copy-start.1
  67.8 1.0 %copy-done.1 = bf16[512,1152]{1,0:T(8,128)(2,1)} copy-done((bf16[512,1152]{1,0:T(8,128)(2,1)}, bf16[512,1152]{1,0:T(8,128)(2,1)S(1)}, u32[]{:S(2)}) %copy-start.1) | copy-done | bytes 1179672
  68.8 3.3 %peer.1 = f32[256,128]{1,0:T(8,128)} custom-call(bf16[512,1152]{1,0:T(8,128)(2,1)} %copy-done, bf16[512,1152]{1,0:T(8,128)(2,1)} %copy-done.1, f32[1,512]{1,0:T(1,128)} %own.1.best_ref), custom_call_target="tpu_custom_call" | custom-call | tf_op jit(solution)/shard_map/peer/pallas_call | solution.py:124
  72.1 23.0 %all_to_all.11 = f32[256,1,128]{2,1,0:T(1,128)} all-to-all(f32[256,1,128]{2,1,0:T(1,128)} %bitcast.7), channel_id=1, replica_groups={{0,1,2,3,8,9,10,11,16,17,18,19,24,25,26,27,32,33,34,35,40,41,42,43,48,4..., dimensions={0} | all-to-all | bytes 262144 | tf_op jit(solution)/shard_map/all_to_all | solution.py:129
  95.1 1.6 %unpack.1 = f32[1,128]{1,0:T(1,128)} custom-call(f32[256,128]{1,0:T(8,128)} %bitcast.8, s32[1,128]{1,0:T(1,128)} %get-tuple-element.8.place_ref), custom_call_target="tpu_custom_call" | custom-call | tf_op jit(solution)/shard_map/unpack/pallas_call | solution.py:132
Async XLA Ops:
  60.0 5.1 %copy-start = (bf16[512,1152]{1,0:T(8,128)(2,1)}, bf16[512,1152]{1,0:T(8,128)(2,1)S(1)}, u32[]{:S(2)}) copy-start(bf16[512,1152]{1,0:T(8,128)(2,1)S(1)} %reshape.24.queries_ref) | copy-start | bytes 3538948
  60.1 7.7 %collective-permute-start = (bf16[512,1152]{1,0:T(8,128)(2,1)S(1)}, bf16[512,1152]{1,0:T(8,128)(2,1)S(1)}, u32[]{:S(2)}, u32[]{:S(2)}) collective-permute-start(bf16[512,1152]{1,0:T(8,128)(2,1)S(1)} %reshape.24.queries_ref), channel_id=1, source_target_pairs={{0,4},{4,0},{8,12},{12,8},{16,20},{20,16},{24,28},{28,24},{32,36},... | collective-permute-start | bytes 3538952 | tf_op jit(solution)/shard_map/ppermute | solution.py:120
  67.8 1.0 %copy-start.1 = (bf16[512,1152]{1,0:T(8,128)(2,1)}, bf16[512,1152]{1,0:T(8,128)(2,1)S(1)}, u32[]{:S(2)}) copy-start(bf16[512,1152]{1,0:T(8,128)(2,1)S(1)} %collective-permute-done.keys_ref) | copy-start | bytes 3538948

commit v2 on v1

--- a/solution.py
+++ b/solution.py
@@ -8,51 +8,59 @@
 EPSILON = 1e-06
 SLOTS = 2
 LANES = 128
+PARAMS = pltpu.CompilerParams(vmem_limit_bytes=16 << 20)
 
 
-def pack_kernel(rows_ref, cluster_ref, rank_ref, send_ref, place_ref):
+def pack_kernel(rows_hbm, cluster_hbm, rank_hbm, send_ref, place_ref, rows_ref, cluster_ref, rank_ref, sems):
+    load_cluster = pltpu.make_async_copy(cluster_hbm, cluster_ref, sems.at[0])
+    load_rank = pltpu.make_async_copy(rank_hbm, rank_ref, sems.at[1])
+    load_rows = pltpu.make_async_copy(rows_hbm, rows_ref, sems.at[2])
+    load_cluster.start()
+    load_rank.start()
+    load_rows.start()
     docs, width = rows_ref.shape
     slots = send_ref.shape[0]
-    values = rows_ref[...].astype(jnp.float32)
-    total = jnp.sum(values * values, axis=1, keepdims=True)
-    unit = (values / jnp.sqrt(total + EPSILON)).astype(jnp.bfloat16)
-    cluster = jnp.broadcast_to(cluster_ref[...], (docs, docs))
-    rank = jnp.broadcast_to(rank_ref[...], (docs, docs))
     row = lax.broadcasted_iota(jnp.int32, (docs, docs), 0)
     col = lax.broadcasted_iota(jnp.int32, (docs, docs), 1)
+    lane = lax.broadcasted_iota(jnp.int32, (docs, LANES), 1)
+    target = lax.broadcasted_iota(jnp.int32, (slots, docs), 0)
+    load_cluster.wait()
+    cluster = jnp.broadcast_to(cluster_ref[...], (docs, docs))
     cluster_col = jnp.sum(jnp.where(row == col, cluster, 0), axis=1, keepdims=True)
-    rank_col = jnp.sum(jnp.where(row == col, rank, 0), axis=1, keepdims=True)
     earlier = (cluster_col == cluster) & (row < col)
     slot = jnp.sum(earlier.astype(jnp.int32), axis=0, keepdims=True)
     place = cluster_ref[...] * SLOTS + slot
     place_ref[...] = place
-    age = 65536 - rank_col
+    onehot = (target == jnp.broadcast_to(place, (slots, docs))).astype(jnp.float32).astype(jnp.bfloat16)
+    load_rank.wait()
+    rank = jnp.broadcast_to(rank_ref[...], (docs, docs))
+    age = 65536 - jnp.sum(jnp.where(row == col, rank, 0), axis=1, keepdims=True)
     high = age // 256
     low = age - high * 256
-    lane = lax.broadcasted_iota(jnp.int32, (docs, LANES), 1)
     digits = jnp.where(lane == 0, high, jnp.where(lane == 1, low, 0))
     digits = digits.astype(jnp.float32).astype(jnp.bfloat16)
-    target = lax.broadcasted_iota(jnp.int32, (slots, docs), 0)
-    onehot = (target == jnp.broadcast_to(place, (slots, docs))).astype(jnp.float32).astype(jnp.bfloat16)
+    send_ref[:, width:] = jnp.dot(onehot, digits, preferred_element_type=jnp.float32).astype(jnp.bfloat16)
+    load_rows.wait()
+    values = rows_ref[...].astype(jnp.float32)
+    total = jnp.sum(values * values, axis=1, keepdims=True)
+    unit = (values / jnp.sqrt(total + EPSILON)).astype(jnp.bfloat16)
     send_ref[:, :width] = jnp.dot(onehot, unit, preferred_element_type=jnp.float32).astype(jnp.bfloat16)
-    send_ref[:, width:] = jnp.dot(onehot, digits, preferred_element_type=jnp.float32).astype(jnp.bfloat16)
 
 
-def ages(rows_ref, width):
-    lane = lax.broadcasted_iota(jnp.int32, (LANES, LANES), 0)
-    weight = jnp.where(lane == 0, 256.0, jnp.where(lane == 1, 1.0, 0.0)).astype(jnp.bfloat16)
-    return weight, rows_ref[:, width:]
+def age_weights(shape, axis):
+    place = lax.broadcasted_iota(jnp.int32, shape, axis)
+    return jnp.where(place == 0, 256.0, jnp.where(place == 1, 1.0, 0.0)).astype(jnp.bfloat16)
 
 
 def best_of(keys_ref, queries_ref, width):
-    weight, key_digits = ages(keys_ref, width)
-    key_age = jnp.dot(key_digits, weight, preferred_element_type=jnp.float32)
-    lane = lax.broadcasted_iota(jnp.int32, (8, LANES), 1)
-    weight_row = jnp.where(lane == 0, 256.0, jnp.where(lane == 1, 1.0, 0.0)).astype(jnp.bfloat16)
     contract = (((1,), (1,)), ((), ()))
-    query_age = lax.dot_general(weight_row, queries_ref[:, width:], contract, preferred_element_type=jnp.float32)
-    count = queries_ref.shape[0]
-    scores = lax.dot_general(keys_ref[:, :width], queries_ref[:, :width], contract, preferred_element_type=jnp.float32)
+    key_age = jnp.dot(keys_ref[:, width:], age_weights((LANES, LANES), 0), preferred_element_type=jnp.float32)
+    query_age = lax.dot_general(
+        age_weights((8, LANES), 1), queries_ref[:, width:], contract, preferred_element_type=jnp.float32
+    )
+    scores = lax.dot_general(
+        keys_ref[:, :width], queries_ref[:, :width], contract, preferred_element_type=jnp.float32
+    )
     allowed = key_age[:, :1] > query_age[:1, :]
     return jnp.max(jnp.where(allowed, scores, -1.0), axis=0, keepdims=True)
 
@@ -111,7 +119,14 @@
                 jax.ShapeDtypeStruct((slots, wide), jnp.bfloat16),
                 jax.ShapeDtypeStruct((1, docs), jnp.int32),
             ),
-            name="pack",
+            in_specs=[pl.BlockSpec(memory_space=pltpu.HBM)] * 3,
+            scratch_shapes=[
+                pltpu.VMEM((docs, width), jnp.bfloat16),
+                pltpu.VMEM((1, docs), jnp.int32),
+                pltpu.VMEM((1, docs), jnp.int32),
+                pltpu.SemaphoreType.DMA((3,)),
+            ],
+            name="pack", compiler_params=PARAMS,
         )(embeddings, cluster_id.reshape(1, docs), rank.reshape(1, docs))
         got = lax.all_to_all(
             send.reshape(clusters, SLOTS, wide), both, 0, 0, axis_index_groups=groups, tiled=True
@@ -119,18 +134,18 @@
         queries = got.reshape(slots, wide)
         keys = lax.ppermute(queries, "docs", partner)
         best = pl.pallas_call(
-            make_own(width), out_shape=jax.ShapeDtypeStruct((1, slots), jnp.float32), name="own"
+            make_own(width), out_shape=jax.ShapeDtypeStruct((1, slots), jnp.float32), name="own", compiler_params=PARAMS
         )(queries)
         scores = pl.pallas_call(
             make_peer(width),
             out_shape=jax.ShapeDtypeStruct((clusters, LANES), jnp.float32),
-            name="peer",
+            name="peer", compiler_params=PARAMS,
         )(queries, keys, best)
         back = lax.all_to_all(
             scores.reshape(clusters, 1, LANES), both, 0, 0, axis_index_groups=groups, tiled=True
         ).reshape(clusters, LANES)
         out = pl.pallas_call(
-            unpack_kernel, out_shape=jax.ShapeDtypeStruct((1, docs), jnp.float32), name="unpack"
+            unpack_kernel, out_shape=jax.ShapeDtypeStruct((1, docs), jnp.float32), name="unpack", compiler_params=PARAMS
         )(back, place)
         return out.reshape(docs)
 

time: 97 us -> 89.4 us (0.922)
  Pallas kernels: 10.1 us -> 3.49 us
  waiting for transfers between devices: 0.01 us -> 1.67 us
  blocking collectives: 77.1 us -> 75.7 us
  local copies, waits for them, and re-layouts: 4.36 us -> 3.22 us
    reshape x1, local copies, waits for them, and re-layouts: 2.85 us -> 0.49 us  [per_device(): send.reshape(clusters, SLOTS, wide)]
    pallas_call x1, Pallas kernels: 3.27 us -> 1 us  [per_device(): pl.pallas_call(make_peer(width), out_shape=jax.ShapeDtypeStruct((clusters...]
    pallas_call x1, Pallas kernels: 2.64 us -> 0.78 us  [per_device(): pl.pallas_call(make_own(width), out_shape=jax.ShapeDtypeStruct((1, slots)...]
    ppermute x1, waiting for transfers between devices: 0.01 us -> 1.67 us  [per_device(): keys = lax.ppermute(queries, 'docs', partner)]
    pallas_call x1, Pallas kernels: 2.61 us -> 1.06 us  [per_device(): pl.pallas_call(pack_kernel, out_shape=(jax.ShapeDtypeStruct((slots, wide)...]
    all_to_all x1, blocking collectives: 23 us -> 21.6 us  [per_device(): lax.all_to_all(scores.reshape(clusters, 1, LANES), both, 0, 0, axis_index...]
    unnamed x4 -> x6, local copies, waits for them, and re-layouts: 1.04 us -> 2.26 us
  transfers between devices with their start and end apart: 1 -> 1, of which waited for: 0 -> 1; matrix products, arithmetic and copies ran while one was open for 0% -> 0% of each run, Pallas kernels for 3% -> 1%
where the time goes in v2:
time: 89.4 us; the launch traced here: 89.2 us
  blocking collectives  75.7 us (85%)
  starting transfers between devices  5.03 us (6%)
  Pallas kernels  3.49 us (4%)
  local copies, waits for them, and re-layouts  3.22 us (4%)
  waiting for transfers between devices  1.67 us (2%)
    all_to_all x1, blocking collectives, per_device(): lax.all_to_all(send.reshape(clusters, SLOTS, wide), both, 0, 0, axis_inde...  54.1 us
    all_to_all x1, blocking collectives, per_device(): lax.all_to_all(scores.reshape(clusters, 1, LANES), both, 0, 0, axis_index...  21.6 us
    ppermute x1, starting transfers between devices, per_device(): keys = lax.ppermute(queries, 'docs', partner)  5.03 us
    unnamed x6, local copies, waits for them, and re-layouts  2.26 us
  transfers between devices with their start and end apart: 1, of which 1 were waited for; matrix products, arithmetic and copies ran while one was open for 0% of the time, Pallas kernels for 1%

profile of v2, /device:TPU:1, one launch (start us, length us, event | category | flops | bytes accessed | tf_op | source)
XLA Modules:
  0.0 89.2 jit_solution(9666952175150424233)
XLA Ops:
  0.0 0.0 copy-start
  0.0 0.9 %copy-done = bf16[128,1024]{1,0:T(8,128)(2,1)S(1)} copy-done((bf16[128,1024]{1,0:T(8,128)(2,1)S(1)}, bf16[128,1024]{1,0:T(8,128)(2,1)}, u32[]{:S(2)}) %copy-start) | copy-done | bytes 262168
  1.0 0.0 copy-start.1
  1.0 0.7 copy-done.1
  1.6 0.0 copy-start.2
  1.6 0.7 copy-done.2
  2.3 1.1 %pack.1 = (bf16[512,1152]{1,0:T(8,128)(2,1)S(1)}, s32[1,128]{1,0:T(1,128)S(1)}) custom-call(bf16[128,1024]{1,0:T(8,128)(2,1)S(1)} %copy-done, s32[1,128]{1,0:T(1,128)S(1)} %bitcast.9, s32[1,128]{1,0:T(1,128)S(1)} %bitcast.10), custom_call_target="tpu_custom_call" | custom-call | tf_op jit(solution)/shard_map/pack/pallas_call | solution.py:116
  3.3 0.5 reshape.23
  3.8 54.1 %all_to_all.10 = bf16[256,2,1152]{2,1,0:T(2,128)(2,1)S(1)} all-to-all(bf16[256,2,1152]{2,1,0:T(2,128)(2,1)S(1)} %reshape.23), channel_id=1, replica_groups={{0,1,2,3,8,9,10,11,16,17,18,19,24,25,26,27,32,33,34,35,40,41,42,43,48,4..., dimensions={0} | all-to-all | bytes 2359296 | tf_op jit(solution)/shard_map/all_to_all | solution.py:131
  57.9 0.5 reshape.24.queries_ref
  58.4 5.0 %collective-permute-start = (bf16[512,1152]{1,0:T(8,128)(2,1)S(1)}, bf16[512,1152]{1,0:T(8,128)(2,1)S(1)}, u32[]{:S(2)}, u32[]{:S(2)}) collective-permute-start(bf16[512,1152]{1,0:T(8,128)(2,1)S(1)} %reshape.24.queries_ref), channel_id=1, source_target_pairs={{0,4},{4,0},{8,12},{12,8},{16,20},{20,16},{24,28},{28,24},{32,36},... | collective-permute-start | bytes 3538952 | tf_op jit(solution)/shard_map/ppermute | solution.py:135
  63.4 0.8 own.1.best_ref
  64.2 1.7 %collective-permute-done.keys_ref = bf16[512,1152]{1,0:T(8,128)(2,1)S(1)} collective-permute-done((bf16[512,1152]{1,0:T(8,128)(2,1)S(1)}, bf16[512,1152]{1,0:T(8,128)(2,1)S(1)}, u32[]{:S(2)}, u32[]{:S(2)}) %collective-permute-start) | collective-permute-done | bytes 1179680 | tf_op jit(solution)/shard_map/ppermute | solution.py:135
  65.9 1.0 %peer.1 = f32[256,128]{1,0:T(8,128)S(1)} custom-call(bf16[512,1152]{1,0:T(8,128)(2,1)S(1)} %reshape.24.queries_ref, bf16[512,1152]{1,0:T(8,128)(2,1)S(1)} %collective-permute-done.keys_ref, f32[1,512]{1,0:T(1,128)S(1)} %own.1.best_ref), custom_call_target="tpu_custom_call" | custom-call | tf_op jit(solution)/shard_map/peer/pallas_call | solution.py:139
  66.9 21.6 %all_to_all.11 = f32[256,1,128]{2,1,0:T(1,128)S(1)} all-to-all(f32[256,1,128]{2,1,0:T(1,128)S(1)} %bitcast.7), channel_id=1, replica_groups={{0,1,2,3,8,9,10,11,16,17,18,19,24,25,26,27,32,33,34,35,40,41,42,43,48,4..., dimensions={0} | all-to-all | bytes 262144 | tf_op jit(solution)/shard_map/all_to_all | solution.py:144
  88.5 0.7 unpack.1
Async XLA Ops:
  0.0 0.9 %copy-start = (bf16[128,1024]{1,0:T(8,128)(2,1)S(1)}, bf16[128,1024]{1,0:T(8,128)(2,1)}, u32[]{:S(2)}) copy-start(bf16[128,1024]{1,0:T(8,128)(2,1)} %rows_hbm.1) | copy-start | bytes 786436
  1.0 0.7 copy-start.1
  1.6 0.7 copy-start.2
  58.4 7.5 %collective-permute-start = (bf16[512,1152]{1,0:T(8,128)(2,1)S(1)}, bf16[512,1152]{1,0:T(8,128)(2,1)S(1)}, u32[]{:S(2)}, u32[]{:S(2)}) collective-permute-start(bf16[512,1152]{1,0:T(8,128)(2,1)S(1)} %reshape.24.queries_ref), channel_id=1, source_target_pairs={{0,4},{4,0},{8,12},{12,8},{16,20},{20,16},{24,28},{28,24},{32,36},... | collective-permute-start | bytes 3538952 | tf_op jit(solution)/shard_map/ppermute | solution.py:135

commit v3 on v1

v3 whole, which is shorter than its diff:
```python
import jax
import jax.numpy as jnp
from jax import lax
from jax.experimental import pallas as pl
from jax.experimental.pallas import tpu as pltpu
from jax.sharding import PartitionSpec as P

EPSILON = 1e-06
CL_DEV = 2
SLOTS = 2
LANES = 128
RANKS = 65536.0
SECOND = 2 * RANKS
SMALL = pltpu.CompilerParams(vmem_limit_bytes=16 << 20)
CONTRACT = (((1,), (1,)), ((), ()))


def pack_kernel(rows_ref, cluster_ref, rank_ref, send_ref, place_ref):
    docs, width = rows_ref.shape
    owners = send_ref.shape[0]
    row = lax.broadcasted_iota(jnp.int32, (docs, docs), 0)
    col = lax.broadcasted_iota(jnp.int32, (docs, docs), 1)
    cluster = jnp.broadcast_to(cluster_ref[...], (docs, docs))
    cluster_col = jnp.sum(jnp.where(row == col, cluster, 0), axis=1, keepdims=True)
    rank = jnp.broadcast_to(rank_ref[...], (docs, docs))
    rank_col = jnp.sum(jnp.where(row == col, rank, 0), axis=1, keepdims=True)
    owner = cluster_ref[...] // CL_DEV
    earlier = (cluster_col // CL_DEV == owner) & (row < col)
    slot = jnp.sum(earlier.astype(jnp.int32), axis=0, keepdims=True)
    place = owner * SLOTS + slot
    place_ref[...] = place
    target = lax.broadcasted_iota(jnp.int32, (owners * SLOTS, docs), 0)
    onehot = (target == place).astype(jnp.float32).astype(jnp.bfloat16)
    age = 65536 - rank_col
    high = age // 256
    low = age - high * 256
    lane = lax.broadcasted_iota(jnp.int32, (docs, LANES), 1)
    digits = jnp.where(lane == 0, high, jnp.where(lane == 1, low, jnp.where(lane == 2, cluster_col % CL_DEV, 0)))
    digits = digits.astype(jnp.float32).astype(jnp.bfloat16)
    codes = jnp.dot(onehot, digits, preferred_element_type=jnp.float32).astype(jnp.bfloat16)
    values = rows_ref[...].astype(jnp.float32)
    total = jnp.sum(values * values, axis=1, keepdims=True)
    unit = (values / jnp.sqrt(total + EPSILON)).astype(jnp.bfloat16)
    rows = jnp.dot(onehot, unit, preferred_element_type=jnp.float32).astype(jnp.bfloat16)
    send_ref[:, :, :width] = rows.reshape(owners, SLOTS, width)
    send_ref[:, :, width:] = codes.reshape(owners, SLOTS, LANES)


def code_weights(shape, axis):
    place = lax.broadcasted_iota(jnp.int32, shape, axis)
    weight = jnp.where(place == 0, 256.0, jnp.where(place == 1, 1.0, jnp.where(place == 2, SECOND, 0.0)))
    return weight.astype(jnp.bfloat16)


def query_codes(queries_ref, width):
    code = lax.dot_general(
        code_weights((8, LANES), 1), queries_ref[:, width:], CONTRACT, preferred_element_type=jnp.float32
    )[:1, :]
    return code, jnp.where(code > RANKS, SECOND + RANKS, RANKS)


def best_of(keys_ref, queries_ref, code, last, width):
    key_code = jnp.dot(keys_ref[:, width:], code_weights((LANES, LANES), 0), preferred_element_type=jnp.float32)
    key_code = key_code[:, :1]
    scores = lax.dot_general(
        keys_ref[:, :width], queries_ref[:, :width], CONTRACT, preferred_element_type=jnp.float32
    )
    allowed = (key_code > code) & (key_code <= last)
    return jnp.max(jnp.where(allowed, scores, -1.0), axis=0, keepdims=True)


def across_kernel(before_ref, after_ref, best_ref):
    width = before_ref.shape[1] - LANES
    code, last = query_codes(before_ref, width)
    best = best_of(after_ref, before_ref, code, last, width)
    best_ref[...] = jnp.broadcast_to(best, best_ref.shape)


def own_kernel(queries_ref, before_ref, after_ref, best_ref):
    width = queries_ref.shape[1] - LANES
    code, last = query_codes(queries_ref, width)
    best = best_of(queries_ref, queries_ref, code, last, width)
    best = jnp.maximum(best, best_of(before_ref, queries_ref, code, last, width))
    best = jnp.maximum(best, best_of(after_ref, queries_ref, code, last, width))
    best_ref[...] = jnp.broadcast_to(best, best_ref.shape)


def spread_kernel(own_ref, across_ref, out_ref):
    best = jnp.maximum(own_ref[:1, :], across_ref[:1, :])
    messages = out_ref.shape[0]
    count = best.shape[1]
    best = jnp.broadcast_to(best, (messages, count))
    row = lax.broadcasted_iota(jnp.int32, (messages, count), 0) * SLOTS
    col = lax.broadcasted_iota(jnp.int32, (messages, count), 1)
    first = jnp.sum(jnp.where(col == row, best, 0.0), axis=1, keepdims=True)
    second = jnp.sum(jnp.where(col == row + 1, best, 0.0), axis=1, keepdims=True)
    lane = lax.broadcasted_iota(jnp.int32, out_ref.shape, 1)
    out_ref[...] = jnp.where(lane == 0, first, second)


def unpack_kernel(scores_ref, place_ref, out_ref):
    owners = scores_ref.shape[0]
    docs = place_ref.shape[1]
    row = lax.broadcasted_iota(jnp.int32, (owners, docs), 0) * SLOTS
    first = jnp.where(place_ref[...] == row, scores_ref[:, 0:1], 0.0)
    second = jnp.where(place_ref[...] == row + 1, scores_ref[:, 1:2], 0.0)
    out_ref[...] = jnp.sum(first + second, axis=0, keepdims=True)


def make_per_device(owners, peers):
    slots = owners * SLOTS
    ahead = [(i, (i + 1) % peers) for i in range(peers)]
    behind = [(i, (i - 1) % peers) for i in range(peers)]
    row = jax.ShapeDtypeStruct((8, slots), jnp.float32)

    def per_device(embeddings, cluster_id, rank):
        docs, width = embeddings.shape
        wide = width + LANES
        send, place = pl.pallas_call(
            pack_kernel,
            out_shape=(
                jax.ShapeDtypeStruct((owners, SLOTS, wide), jnp.bfloat16),
                jax.ShapeDtypeStruct((1, docs), jnp.int32),
            ),
            name="pack",
        )(embeddings, cluster_id.reshape(1, docs), rank.reshape(1, docs))
        queries = lax.all_to_all(send, "docs", 0, 0, tiled=True).reshape(slots, wide)
        before = lax.ppermute(queries, "split", ahead)
        after = lax.ppermute(queries, "split", behind)
        across = pl.pallas_call(across_kernel, out_shape=row, compiler_params=SMALL, name="across")(before, after)
        across = lax.ppermute(across, "split", behind)
        own = pl.pallas_call(own_kernel, out_shape=row, compiler_params=SMALL, name="own")(queries, before, after)
        scores = pl.pallas_call(
            spread_kernel,
            out_shape=jax.ShapeDtypeStruct((owners, LANES), jnp.float32),
            compiler_params=SMALL,
            name="spread",
        )(own, across)
        back = lax.all_to_all(scores.reshape(owners, 1, LANES), "docs", 0, 0, tiled=True)
        out = pl.pallas_call(
            unpack_kernel,
            out_shape=jax.ShapeDtypeStruct((1, docs), jnp.float32),
            compiler_params=SMALL,
            name="unpack",
        )(back.reshape(owners, LANES), place)
        return out.reshape(docs)

    return per_device


def solution(mesh):
    placed = (P(("docs", "split"), None), P(("docs", "split")), P(("docs", "split")))
    assert mesh.shape["split"] == 4
    per_device = make_per_device(mesh.shape["docs"], mesh.shape["split"])
    return jax.shard_map(
        per_device, mesh=mesh, in_specs=placed, out_specs=P(("docs", "split")), check_vma=False
    )
```

time: 97 us -> 90.1 us (0.929)
  blocking collectives: 77.1 us -> 61 us
  waiting for transfers between devices: 0.01 us -> 15.5 us
  Pallas kernels: 10.1 us -> 4.18 us
  local copies, waits for them, and re-layouts: 4.36 us -> 0.88 us
  starting transfers between devices: 5.03 us -> 8.23 us
    all_to_all x2, blocking collectives: 77.1 us -> 61 us  [the longest x1 39.3 us: per_device(): lax.all_to_all(send, 'docs', 0, 0, tiled=True).reshape(slots, wide)]
    ppermute x1 -> x3, waiting for transfers between devices: 0.01 us -> 15.5 us  [the longest x1 8.68 us: per_device(): after = lax.ppermute(queries, 'split', behind)]
    pallas_call x3 -> x4, Pallas kernels: 8.52 us -> 3.56 us  [the longest x1 2.35 us: per_device(): pl.pallas_call(pack_kernel, out_shape=(jax.ShapeDtypeStruct((owners, SLOT...]
    ppermute x1 -> x3, starting transfers between devices: 5.03 us -> 8.23 us  [the longest x1 4.39 us: per_device(): after = lax.ppermute(queries, 'split', behind)]
    reshape x2 -> x1, local copies, waits for them, and re-layouts: 3.32 us -> 0.22 us  [per_device(): lax.all_to_all(send, 'docs', 0, 0, tiled=True).reshape(slots, wide)]
  transfers between devices with their start and end apart: 1 -> 3, of which waited for: 0 -> 3; matrix products, arithmetic and copies ran while one was open for 0% -> 0% of each run, Pallas kernels for 3% -> 1%
where the time goes in v3:
time: 90.1 us; the launch traced here: 89.8 us
  blocking collectives  61 us (68%)
  waiting for transfers between devices  15.5 us (17%)
  starting transfers between devices  8.23 us (9%)
  Pallas kernels  4.18 us (5%)
    all_to_all x1, blocking collectives, per_device(): lax.all_to_all(send, 'docs', 0, 0, tiled=True).reshape(slots, wide)  39.3 us
    all_to_all x1, blocking collectives, per_device(): lax.all_to_all(scores.reshape(owners, 1, LANES), 'docs', 0, 0, tiled=True)  21.7 us
    ppermute x1, waiting for transfers between devices, per_device(): after = lax.ppermute(queries, 'split', behind)  8.68 us
    ppermute x1, waiting for transfers between devices, per_device(): before = lax.ppermute(queries, 'split', ahead)  5.05 us
    ppermute x1, starting transfers between devices, per_device(): after = lax.ppermute(queries, 'split', behind)  4.39 us
    pallas_call x1, Pallas kernels, per_device(): pl.pallas_call(pack_kernel, out_shape=(jax.ShapeDtypeStruct((owners, SLOT...  2.35 us
    ppermute x1, starting transfers between devices, per_device(): before = lax.ppermute(queries, 'split', ahead)  1.92 us
    ppermute x1, starting transfers between devices, per_device(): across = lax.ppermute(across, 'split', behind)  1.92 us
  transfers between devices with their start and end apart: 3, of which 3 were waited for; matrix products, arithmetic and copies ran while one was open for 0% of the time, Pallas kernels for 1%

profile of v3, /device:TPU:1, one launch (start us, length us, event | category | flops | bytes accessed | tf_op | source)
XLA Modules:
  0.0 89.8 jit_solution(8837935660476919056)
XLA Ops:
  0.0 2.4 %pack.1 = (bf16[128,2,1152]{2,1,0:T(2,128)(2,1)}, s32[1,128]{1,0:T(1,128)}) custom-call(bf16[128,1024]{1,0:T(8,128)(2,1)} %rows_ref.1, s32[1,128]{1,0:T(1,128)} %bitcast.9, s32[1,128]{1,0:T(1,128)} %bitcast.10), custom_call_target="tpu_custom_call" | custom-call | tf_op jit(solution)/shard_map/pack/pallas_call | solution.py:119
  2.4 39.3 %all_to_all.10 = bf16[128,2,1152]{2,1,0:T(2,128)(2,1)S(1)} all-to-all(bf16[128,2,1152]{2,1,0:T(2,128)(2,1)} %get-tuple-element.7), channel_id=1, replica_groups=mesh['docs'=128,'split'=4] {'docs'}, dimensions={0} | all-to-all | bytes 1179648 | tf_op jit(solution)/shard_map/all_to_all | solution.py:127
  41.6 0.2 reshape.20.queries_ref
  41.9 4.4 %collective-permute-start.1 = (bf16[256,1152]{1,0:T(8,128)(2,1)S(1)}, bf16[256,1152]{1,0:T(8,128)(2,1)S(1)}, u32[]{:S(2)}, u32[]{:S(2)}) collective-permute-start(bf16[256,1152]{1,0:T(8,128)(2,1)S(1)} %reshape.20.queries_ref), channel_id=1, source_target_pairs={{0,3},{1,0},{2,1},{3,2},{4,7},{5,4},{6,5},{7,6},{8,11},{9,8},{10,9... | collective-permute-start | bytes 1769480 | tf_op jit(solution)/shard_map/ppermute | solution.py:129
  46.3 1.9 %collective-permute-start = (bf16[256,1152]{1,0:T(8,128)(2,1)S(1)}, bf16[256,1152]{1,0:T(8,128)(2,1)S(1)}, u32[]{:S(2)}, u32[]{:S(2)}) collective-permute-start(bf16[256,1152]{1,0:T(8,128)(2,1)S(1)} %reshape.20.queries_ref), channel_id=1, source_target_pairs={{0,1},{1,2},{2,3},{3,0},{4,5},{5,6},{6,7},{7,4},{8,9},{9,10},{10,1... | collective-permute-start | bytes 1769480 | tf_op jit(solution)/shard_map/ppermute | solution.py:128
  48.2 8.7 %collective-permute-done.1.after_ref = bf16[256,1152]{1,0:T(8,128)(2,1)S(1)} collective-permute-done((bf16[256,1152]{1,0:T(8,128)(2,1)S(1)}, bf16[256,1152]{1,0:T(8,128)(2,1)S(1)}, u32[]{:S(2)}, u32[]{:S(2)}) %collective-permute-start.1) | collective-permute-done | bytes 589856 | tf_op jit(solution)/shard_map/ppermute | solution.py:129
  56.9 5.0 %collective-permute-done.before_ref = bf16[256,1152]{1,0:T(8,128)(2,1)S(1)} collective-permute-done((bf16[256,1152]{1,0:T(8,128)(2,1)S(1)}, bf16[256,1152]{1,0:T(8,128)(2,1)S(1)}, u32[]{:S(2)}, u32[]{:S(2)}) %collective-permute-start) | collective-permute-done | bytes 589856 | tf_op jit(solution)/shard_map/ppermute | solution.py:128
  61.9 0.4 across.1
  62.3 1.9 %collective-permute-start.2 = (f32[8,256]{1,0:T(8,128)S(1)}, f32[8,256]{1,0:T(8,128)S(1)}, u32[]{:S(2)}, u32[]{:S(2)}) collective-permute-start(f32[8,256]{1,0:T(8,128)S(1)} %across.1), channel_id=1, source_target_pairs={{0,3},{1,0},{2,1},{3,2},{4,7},{5,4},{6,5},{7,6},{8,11},{9,8},{10,9... | collective-permute-start | bytes 24584 | tf_op jit(solution)/shard_map/ppermute | solution.py:131
  64.2 0.7 own.1.own_ref
  65.0 1.7 %collective-permute-done.2.across_ref = f32[8,256]{1,0:T(8,128)S(1)} collective-permute-done((f32[8,256]{1,0:T(8,128)S(1)}, f32[8,256]{1,0:T(8,128)S(1)}, u32[]{:S(2)}, u32[]{:S(2)}) %collective-permute-start.2) | collective-permute-done | bytes 8224 | tf_op jit(solution)/shard_map/ppermute | solution.py:131
  66.7 0.1 spread.1
  66.8 21.7 %all_to_all.11 = f32[128,1,128]{2,1,0:T(1,128)S(1)} all-to-all(f32[128,1,128]{2,1,0:T(1,128)S(1)} %bitcast.7), channel_id=1, replica_groups=mesh['docs'=128,'split'=4] {'docs'}, dimensions={0} | all-to-all | bytes 131072 | tf_op jit(solution)/shard_map/all_to_all | solution.py:139
  88.5 0.0 copy-start
  88.5 0.7 copy-done
  89.2 0.6 unpack.1
Async XLA Ops:
  41.9 15.0 %collective-permute-start.1 = (bf16[256,1152]{1,0:T(8,128)(2,1)S(1)}, bf16[256,1152]{1,0:T(8,128)(2,1)S(1)}, u32[]{:S(2)}, u32[]{:S(2)}) collective-permute-start(bf16[256,1152]{1,0:T(8,128)(2,1)S(1)} %reshape.20.queries_ref), channel_id=1, source_target_pairs={{0,3},{1,0},{2,1},{3,2},{4,7},{5,4},{6,5},{7,6},{8,11},{9,8},{10,9... | collective-permute-start | bytes 1769480 | tf_op jit(solution)/shard_map/ppermute | solution.py:129
  46.3 15.7 %collective-permute-start = (bf16[256,1152]{1,0:T(8,128)(2,1)S(1)}, bf16[256,1152]{1,0:T(8,128)(2,1)S(1)}, u32[]{:S(2)}, u32[]{:S(2)}) collective-permute-start(bf16[256,1152]{1,0:T(8,128)(2,1)S(1)} %reshape.20.queries_ref), channel_id=1, source_target_pairs={{0,1},{1,2},{2,3},{3,0},{4,5},{5,6},{6,7},{7,4},{8,9},{9,10},{10,1... | collective-permute-start | bytes 1769480 | tf_op jit(solution)/shard_map/ppermute | solution.py:128
  62.3 4.4 %collective-permute-start.2 = (f32[8,256]{1,0:T(8,128)S(1)}, f32[8,256]{1,0:T(8,128)S(1)}, u32[]{:S(2)}, u32[]{:S(2)}) collective-permute-start(f32[8,256]{1,0:T(8,128)S(1)} %across.1), channel_id=1, source_target_pairs={{0,3},{1,0},{2,1},{3,2},{4,7},{5,4},{6,5},{7,6},{8,11},{9,8},{10,9... | collective-permute-start | bytes 24584 | tf_op jit(solution)/shard_map/ppermute | solution.py:131
  88.5 0.7 copy-start

commit v4 on v2

--- a/solution.py
+++ b/solution.py
@@ -19,7 +19,8 @@
     load_rank.start()
     load_rows.start()
     docs, width = rows_ref.shape
-    slots = send_ref.shape[0]
+    clusters = send_ref.shape[0]
+    slots = clusters * SLOTS
     row = lax.broadcasted_iota(jnp.int32, (docs, docs), 0)
     col = lax.broadcasted_iota(jnp.int32, (docs, docs), 1)
     lane = lax.broadcasted_iota(jnp.int32, (docs, LANES), 1)
@@ -39,12 +40,14 @@
     low = age - high * 256
     digits = jnp.where(lane == 0, high, jnp.where(lane == 1, low, 0))
     digits = digits.astype(jnp.float32).astype(jnp.bfloat16)
-    send_ref[:, width:] = jnp.dot(onehot, digits, preferred_element_type=jnp.float32).astype(jnp.bfloat16)
+    digits = jnp.dot(onehot, digits, preferred_element_type=jnp.float32).astype(jnp.bfloat16)
+    send_ref[:, :, width:] = digits.reshape(clusters, SLOTS, LANES)
     load_rows.wait()
     values = rows_ref[...].astype(jnp.float32)
     total = jnp.sum(values * values, axis=1, keepdims=True)
     unit = (values / jnp.sqrt(total + EPSILON)).astype(jnp.bfloat16)
-    send_ref[:, :width] = jnp.dot(onehot, unit, preferred_element_type=jnp.float32).astype(jnp.bfloat16)
+    rows = jnp.dot(onehot, unit, preferred_element_type=jnp.float32).astype(jnp.bfloat16)
+    send_ref[:, :, :width] = rows.reshape(clusters, SLOTS, width)
 
 
 def age_weights(shape, axis):
@@ -116,7 +119,7 @@
         send, place = pl.pallas_call(
             pack_kernel,
             out_shape=(
-                jax.ShapeDtypeStruct((slots, wide), jnp.bfloat16),
+                jax.ShapeDtypeStruct((clusters, SLOTS, wide), jnp.bfloat16),
                 jax.ShapeDtypeStruct((1, docs), jnp.int32),
             ),
             in_specs=[pl.BlockSpec(memory_space=pltpu.HBM)] * 3,
@@ -127,9 +130,13 @@
                 pltpu.SemaphoreType.DMA((3,)),
             ],
             name="pack", compiler_params=PARAMS,
-        )(embeddings, cluster_id.reshape(1, docs), rank.reshape(1, docs))
+        )(
+            pltpu.with_memory_space_constraint(embeddings, pltpu.HBM),
+            pltpu.with_memory_space_constraint(cluster_id.reshape(1, docs), pltpu.HBM),
+            pltpu.with_memory_space_constraint(rank.reshape(1, docs), pltpu.HBM),
+        )
         got = lax.all_to_all(
-            send.reshape(clusters, SLOTS, wide), both, 0, 0, axis_index_groups=groups, tiled=True
+            send, both, 0, 0, axis_index_groups=groups, tiled=True
         )
         queries = got.reshape(slots, wide)
         keys = lax.ppermute(queries, "docs", partner)

time: 89.4 us -> 87.3 us (0.977)
  local copies, waits for them, and re-layouts: 3.22 us -> 0.47 us
    unnamed x6 -> x0, local copies, waits for them, and re-layouts: 2.26 us -> none
where the time goes in v4:
time: 87.3 us; the launch traced here: 87.1 us
  blocking collectives  75.7 us (87%)
  starting transfers between devices  5.03 us (6%)
  Pallas kernels  4.19 us (5%)
  waiting for transfers between devices  1.67 us (2%)
    all_to_all x1, blocking collectives, per_device(): got = lax.all_to_all(send, both, 0, 0, axis_index_groups=groups, tiled=True)  54.1 us
    all_to_all x1, blocking collectives, per_device(): lax.all_to_all(scores.reshape(clusters, 1, LANES), both, 0, 0, axis_index...  21.6 us
    ppermute x1, starting transfers between devices, per_device(): keys = lax.ppermute(queries, 'docs', partner)  5.03 us
    pallas_call x1, Pallas kernels, per_device(): pl.pallas_call(pack_kernel, out_shape=(jax.ShapeDtypeStruct((clusters, SL...  1.76 us
  transfers between devices with their start and end apart: 1, of which 1 were waited for; matrix products, arithmetic and copies ran while one was open for 0% of the time, Pallas kernels for 1%

profile of v4, /device:TPU:1, one launch (start us, length us, event | category | flops | bytes accessed | tf_op | source)
XLA Modules:
  0.0 87.1 jit_solution(3283854050127922880)
XLA Ops:
  0.0 1.8 %pack.1 = (bf16[256,2,1152]{2,1,0:T(2,128)(2,1)S(1)}, s32[1,128]{1,0:T(1,128)S(1)}) custom-call(bf16[128,1024]{1,0:T(8,128)(2,1)} %rows_hbm.1, s32[1,128]{1,0:T(1,128)} %bitcast.9, s32[1,128]{1,0:T(1,128)} %bitcast.10), custom_call_target="tpu_custom_call" | custom-call | tf_op jit(solution)/shard_map/pack/pallas_call | solution.py:119
  1.8 54.1 %all_to_all.10 = bf16[256,2,1152]{2,1,0:T(2,128)(2,1)S(1)} all-to-all(bf16[256,2,1152]{2,1,0:T(2,128)(2,1)S(1)} %get-tuple-element.7), channel_id=1, replica_groups={{0,1,2,3,8,9,10,11,16,17,18,19,24,25,26,27,32,33,34,35,40,41,42,43,48,4..., dimensions={0} | all-to-all | bytes 2359296 | tf_op jit(solution)/shard_map/all_to_all | solution.py:138
  55.9 0.5 reshape.20.queries_ref
  56.3 5.0 %collective-permute-start = (bf16[512,1152]{1,0:T(8,128)(2,1)S(1)}, bf16[512,1152]{1,0:T(8,128)(2,1)S(1)}, u32[]{:S(2)}, u32[]{:S(2)}) collective-permute-start(bf16[512,1152]{1,0:T(8,128)(2,1)S(1)} %reshape.20.queries_ref), channel_id=1, source_target_pairs={{0,4},{4,0},{8,12},{12,8},{16,20},{20,16},{24,28},{28,24},{32,36},... | collective-permute-start | bytes 3538952 | tf_op jit(solution)/shard_map/ppermute | solution.py:142
  61.4 0.8 own.1.best_ref
  62.2 1.7 %collective-permute-done.keys_ref = bf16[512,1152]{1,0:T(8,128)(2,1)S(1)} collective-permute-done((bf16[512,1152]{1,0:T(8,128)(2,1)S(1)}, bf16[512,1152]{1,0:T(8,128)(2,1)S(1)}, u32[]{:S(2)}, u32[]{:S(2)}) %collective-permute-start) | collective-permute-done | bytes 1179680 | tf_op jit(solution)/shard_map/ppermute | solution.py:142
  63.8 1.0 %peer.1 = f32[256,128]{1,0:T(8,128)S(1)} custom-call(bf16[512,1152]{1,0:T(8,128)(2,1)S(1)} %reshape.20.queries_ref, bf16[512,1152]{1,0:T(8,128)(2,1)S(1)} %collective-permute-done.keys_ref, f32[1,512]{1,0:T(1,128)S(1)} %own.1.best_ref), custom_call_target="tpu_custom_call" | custom-call | tf_op jit(solution)/shard_map/peer/pallas_call | solution.py:146
  64.8 21.6 %all_to_all.11 = f32[256,1,128]{2,1,0:T(1,128)S(1)} all-to-all(f32[256,1,128]{2,1,0:T(1,128)S(1)} %bitcast.7), channel_id=1, replica_groups={{0,1,2,3,8,9,10,11,16,17,18,19,24,25,26,27,32,33,34,35,40,41,42,43,48,4..., dimensions={0} | all-to-all | bytes 262144 | tf_op jit(solution)/shard_map/all_to_all | solution.py:151
  86.4 0.7 unpack.1
Async XLA Ops:
  56.3 7.5 %collective-permute-start = (bf16[512,1152]{1,0:T(8,128)(2,1)S(1)}, bf16[512,1152]{1,0:T(8,128)(2,1)S(1)}, u32[]{:S(2)}, u32[]{:S(2)}) collective-permute-start(bf16[512,1152]{1,0:T(8,128)(2,1)S(1)} %reshape.20.queries_ref), channel_id=1, source_target_pairs={{0,4},{4,0},{8,12},{12,8},{16,20},{20,16},{24,28},{28,24},{32,36},... | collective-permute-start | bytes 3538952 | tf_op jit(solution)/shard_map/ppermute | solution.py:142

commit v5 on v3

--- a/solution.py
+++ b/solution.py
@@ -15,35 +15,43 @@
 CONTRACT = (((1,), (1,)), ((), ()))
 
 
-def pack_kernel(rows_ref, cluster_ref, rank_ref, send_ref, place_ref):
+def pack_kernel(rows_hbm, cluster_hbm, rank_hbm, send_ref, place_ref, rows_ref, cluster_ref, rank_ref, sems):
+    load_cluster = pltpu.make_async_copy(cluster_hbm, cluster_ref, sems.at[0])
+    load_rank = pltpu.make_async_copy(rank_hbm, rank_ref, sems.at[1])
+    load_rows = pltpu.make_async_copy(rows_hbm, rows_ref, sems.at[2])
+    load_cluster.start()
+    load_rank.start()
+    load_rows.start()
     docs, width = rows_ref.shape
     owners = send_ref.shape[0]
     row = lax.broadcasted_iota(jnp.int32, (docs, docs), 0)
     col = lax.broadcasted_iota(jnp.int32, (docs, docs), 1)
+    lane = lax.broadcasted_iota(jnp.int32, (docs, LANES), 1)
+    target = lax.broadcasted_iota(jnp.int32, (owners * SLOTS, docs), 0)
+    load_cluster.wait()
     cluster = jnp.broadcast_to(cluster_ref[...], (docs, docs))
     cluster_col = jnp.sum(jnp.where(row == col, cluster, 0), axis=1, keepdims=True)
-    rank = jnp.broadcast_to(rank_ref[...], (docs, docs))
-    rank_col = jnp.sum(jnp.where(row == col, rank, 0), axis=1, keepdims=True)
     owner = cluster_ref[...] // CL_DEV
     earlier = (cluster_col // CL_DEV == owner) & (row < col)
     slot = jnp.sum(earlier.astype(jnp.int32), axis=0, keepdims=True)
     place = owner * SLOTS + slot
     place_ref[...] = place
-    target = lax.broadcasted_iota(jnp.int32, (owners * SLOTS, docs), 0)
     onehot = (target == place).astype(jnp.float32).astype(jnp.bfloat16)
-    age = 65536 - rank_col
+    load_rank.wait()
+    rank = jnp.broadcast_to(rank_ref[...], (docs, docs))
+    age = 65536 - jnp.sum(jnp.where(row == col, rank, 0), axis=1, keepdims=True)
     high = age // 256
     low = age - high * 256
-    lane = lax.broadcasted_iota(jnp.int32, (docs, LANES), 1)
     digits = jnp.where(lane == 0, high, jnp.where(lane == 1, low, jnp.where(lane == 2, cluster_col % CL_DEV, 0)))
     digits = digits.astype(jnp.float32).astype(jnp.bfloat16)
     codes = jnp.dot(onehot, digits, preferred_element_type=jnp.float32).astype(jnp.bfloat16)
+    send_ref[:, :, width:] = codes.reshape(owners, SLOTS, LANES)
+    load_rows.wait()
     values = rows_ref[...].astype(jnp.float32)
     total = jnp.sum(values * values, axis=1, keepdims=True)
     unit = (values / jnp.sqrt(total + EPSILON)).astype(jnp.bfloat16)
     rows = jnp.dot(onehot, unit, preferred_element_type=jnp.float32).astype(jnp.bfloat16)
     send_ref[:, :, :width] = rows.reshape(owners, SLOTS, width)
-    send_ref[:, :, width:] = codes.reshape(owners, SLOTS, LANES)
 
 
 def code_weights(shape, axis):
@@ -107,10 +115,32 @@
     out_ref[...] = jnp.sum(first + second, axis=0, keepdims=True)
 
 
-def make_per_device(owners, peers):
+RING = {(0, 0): 0, (0, 1): 1, (1, 1): 2, (1, 0): 3}
+
+
+def layout(side_y, side_z, side_x):
+    table = {}
+    for y in range(side_y):
+        for z in range(side_z):
+            for core in range(2):
+                sy, sz = (y + core) % side_y, (z + core) % side_z
+                square = (sy // 2) * (side_z // 2) + sz // 2
+                for x in range(side_x):
+                    owner = (x * (side_y // 2) * (side_z // 2) + square) * 2 + core
+                    device = ((y * side_z + z) * 2 + core) * side_x + x
+                    table[RING[sy % 2, sz % 2], owner] = device
+    owners = max(owner for _, owner in table) + 1
+    groups = [[table[member, owner] for owner in range(owners)] for member in range(4)]
+    ahead = [(table[m, o], table[(m + 1) % 4, o]) for m in range(4) for o in range(owners)]
+    behind = [(b, a) for a, b in ahead]
+    return owners, groups, ahead, behind
+
+
+def make_per_device(docs_axis, split_axis):
+    side = round((docs_axis // 2) ** 0.5)
+    owners, groups, ahead, behind = layout(side, side, split_axis)
     slots = owners * SLOTS
-    ahead = [(i, (i + 1) % peers) for i in range(peers)]
-    behind = [(i, (i - 1) % peers) for i in range(peers)]
+    both = ("docs", "split")
     row = jax.ShapeDtypeStruct((8, slots), jnp.float32)
 
     def per_device(embeddings, cluster_id, rank):
@@ -122,13 +152,26 @@
                 jax.ShapeDtypeStruct((owners, SLOTS, wide), jnp.bfloat16),
                 jax.ShapeDtypeStruct((1, docs), jnp.int32),
             ),
+            in_specs=[pl.BlockSpec(memory_space=pltpu.HBM)] * 3,
+            scratch_shapes=[
+                pltpu.VMEM((docs, width), jnp.bfloat16),
+                pltpu.VMEM((1, docs), jnp.int32),
+                pltpu.VMEM((1, docs), jnp.int32),
+                pltpu.SemaphoreType.DMA((3,)),
+            ],
+            compiler_params=SMALL,
             name="pack",
-        )(embeddings, cluster_id.reshape(1, docs), rank.reshape(1, docs))
-        queries = lax.all_to_all(send, "docs", 0, 0, tiled=True).reshape(slots, wide)
-        before = lax.ppermute(queries, "split", ahead)
-        after = lax.ppermute(queries, "split", behind)
+        )(
+            pltpu.with_memory_space_constraint(embeddings, pltpu.HBM),
+            pltpu.with_memory_space_constraint(cluster_id.reshape(1, docs), pltpu.HBM),
+            pltpu.with_memory_space_constraint(rank.reshape(1, docs), pltpu.HBM),
+        )
+        got = lax.all_to_all(send, both, 0, 0, axis_index_groups=groups, tiled=True)
+        queries = got.reshape(slots, wide)
+        before = lax.ppermute(queries, both, ahead)
+        after = lax.ppermute(queries, both, behind)
         across = pl.pallas_call(across_kernel, out_shape=row, compiler_params=SMALL, name="across")(before, after)
-        across = lax.ppermute(across, "split", behind)
+        across = lax.ppermute(across, both, behind)
         own = pl.pallas_call(own_kernel, out_shape=row, compiler_params=SMALL, name="own")(queries, before, after)
         scores = pl.pallas_call(
             spread_kernel,
@@ -136,7 +179,9 @@
             compiler_params=SMALL,
             name="spread",
         )(own, across)
-        back = lax.all_to_all(scores.reshape(owners, 1, LANES), "docs", 0, 0, tiled=True)
+        back = lax.all_to_all(
+            scores.reshape(owners, 1, LANES), both, 0, 0, axis_index_groups=groups, tiled=True
+        )
         out = pl.pallas_call(
             unpack_kernel,
             out_shape=jax.ShapeDtypeStruct((1, docs), jnp.float32),
@@ -150,7 +195,6 @@
 
 def solution(mesh):
     placed = (P(("docs", "split"), None), P(("docs", "split")), P(("docs", "split")))
-    assert mesh.shape["split"] == 4
     per_device = make_per_device(mesh.shape["docs"], mesh.shape["split"])
     return jax.shard_map(
         per_device, mesh=mesh, in_specs=placed, out_specs=P(("docs", "split")), check_vma=False

time: 90.1 us -> 88 us (0.977)
  waiting for transfers between devices: 15.5 us -> 10.9 us
  blocking collectives: 61 us -> 64.3 us
    ppermute x3, waiting for transfers between devices: 15.5 us -> 10.9 us  [the longest x1 5.33 us: per_device(): after = lax.ppermute(queries, both, behind)]
    all_to_all x2, blocking collectives: 61 us -> 64.3 us  [the longest x1 44.2 us: per_device(): got = lax.all_to_all(send, both, 0, 0, axis_index_groups=groups, tiled=True)]
where the time goes in v5:
time: 88 us; the launch traced here: 87.8 us
  blocking collectives  64.3 us (73%)
  waiting for transfers between devices  10.9 us (12%)
  starting transfers between devices  8.8 us (10%)
  Pallas kernels  3.4 us (4%)
    all_to_all x1, blocking collectives, per_device(): got = lax.all_to_all(send, both, 0, 0, axis_index_groups=groups, tiled=True)  44.2 us
    all_to_all x1, blocking collectives, per_device(): lax.all_to_all(scores.reshape(owners, 1, LANES), both, 0, 0, axis_index_g...  20.2 us
    ppermute x1, waiting for transfers between devices, per_device(): after = lax.ppermute(queries, both, behind)  5.33 us
    ppermute x1, starting transfers between devices, per_device(): before = lax.ppermute(queries, both, ahead)  3.45 us
    ppermute x1, waiting for transfers between devices, per_device(): before = lax.ppermute(queries, both, ahead)  3.06 us
    ppermute x1, starting transfers between devices, per_device(): after = lax.ppermute(queries, both, behind)  3.05 us
    ppermute x1, waiting for transfers between devices, per_device(): across = lax.ppermute(across, both, behind)  2.55 us
    ppermute x1, starting transfers between devices, per_device(): across = lax.ppermute(across, both, behind)  2.31 us
  transfers between devices with their start and end apart: 3, of which 3 were waited for; matrix products, arithmetic and copies ran while one was open for 0% of the time, Pallas kernels for 1%

profile of v5, /device:TPU:1, one launch (start us, length us, event | category | flops | bytes accessed | tf_op | source)
XLA Modules:
  0.0 87.8 jit_solution(8109624254637280234)
XLA Ops:
  0.0 1.6 %pack.1 = (bf16[128,2,1152]{2,1,0:T(2,128)(2,1)S(1)}, s32[1,128]{1,0:T(1,128)S(1)}) custom-call(bf16[128,1024]{1,0:T(8,128)(2,1)} %rows_hbm.1, s32[1,128]{1,0:T(1,128)} %bitcast.9, s32[1,128]{1,0:T(1,128)} %bitcast.10), custom_call_target="tpu_custom_call" | custom-call | tf_op jit(solution)/shard_map/pack/pallas_call | solution.py:149
  1.6 44.2 %all_to_all.10 = bf16[128,2,1152]{2,1,0:T(2,128)(2,1)S(1)} all-to-all(bf16[128,2,1152]{2,1,0:T(2,128)(2,1)S(1)} %get-tuple-element.7), channel_id=1, replica_groups={{0,508,16,460,32,476,48,492,128,124,144,76,160,92,176,108,256,252,272,2..., dimensions={0} | all-to-all | bytes 1179648 | tf_op jit(solution)/shard_map/all_to_all | solution.py:169
  45.7 0.2 reshape.20.queries_ref
  46.0 3.0 %collective-permute-start.1 = (bf16[256,1152]{1,0:T(8,128)(2,1)S(1)}, bf16[256,1152]{1,0:T(8,128)(2,1)S(1)}, u32[]{:S(2)}, u32[]{:S(2)}) collective-permute-start(bf16[256,1152]{1,0:T(8,128)(2,1)S(1)} %reshape.20.queries_ref), channel_id=1, source_target_pairs={{8,0},{452,508},{24,16},{468,460},{40,32},{484,476},{56,48},{500,4... | collective-permute-start | bytes 1769480 | tf_op jit(solution)/shard_map/ppermute | solution.py:172
  49.0 3.4 %collective-permute-start = (bf16[256,1152]{1,0:T(8,128)(2,1)S(1)}, bf16[256,1152]{1,0:T(8,128)(2,1)S(1)}, u32[]{:S(2)}, u32[]{:S(2)}) collective-permute-start(bf16[256,1152]{1,0:T(8,128)(2,1)S(1)} %reshape.20.queries_ref), channel_id=1, source_target_pairs={{0,8},{508,452},{16,24},{460,468},{32,40},{476,484},{48,56},{492,5... | collective-permute-start | bytes 1769480 | tf_op jit(solution)/shard_map/ppermute | solution.py:171
  52.5 5.3 %collective-permute-done.1.after_ref = bf16[256,1152]{1,0:T(8,128)(2,1)S(1)} collective-permute-done((bf16[256,1152]{1,0:T(8,128)(2,1)S(1)}, bf16[256,1152]{1,0:T(8,128)(2,1)S(1)}, u32[]{:S(2)}, u32[]{:S(2)}) %collective-permute-start.1) | collective-permute-done | bytes 589856 | tf_op jit(solution)/shard_map/ppermute | solution.py:172
  57.8 3.1 %collective-permute-done.before_ref = bf16[256,1152]{1,0:T(8,128)(2,1)S(1)} collective-permute-done((bf16[256,1152]{1,0:T(8,128)(2,1)S(1)}, bf16[256,1152]{1,0:T(8,128)(2,1)S(1)}, u32[]{:S(2)}, u32[]{:S(2)}) %collective-permute-start) | collective-permute-done | bytes 589856 | tf_op jit(solution)/shard_map/ppermute | solution.py:171
  60.9 0.4 across.1
  61.2 2.3 %collective-permute-start.2 = (f32[8,256]{1,0:T(8,128)S(1)}, f32[8,256]{1,0:T(8,128)S(1)}, u32[]{:S(2)}, u32[]{:S(2)}) collective-permute-start(f32[8,256]{1,0:T(8,128)S(1)} %across.1), channel_id=1, source_target_pairs={{8,0},{452,508},{24,16},{468,460},{40,32},{484,476},{56,48},{500,4... | collective-permute-start | bytes 24584 | tf_op jit(solution)/shard_map/ppermute | solution.py:174
  63.5 0.7 own.1.own_ref
  64.3 2.6 %collective-permute-done.2.across_ref = f32[8,256]{1,0:T(8,128)S(1)} collective-permute-done((f32[8,256]{1,0:T(8,128)S(1)}, f32[8,256]{1,0:T(8,128)S(1)}, u32[]{:S(2)}, u32[]{:S(2)}) %collective-permute-start.2) | collective-permute-done | bytes 8224 | tf_op jit(solution)/shard_map/ppermute | solution.py:174
  66.8 0.1 spread.1
  67.0 20.2 %all_to_all.11 = f32[128,1,128]{2,1,0:T(1,128)S(1)} all-to-all(f32[128,1,128]{2,1,0:T(1,128)S(1)} %bitcast.7), channel_id=1, replica_groups={{0,508,16,460,32,476,48,492,128,124,144,76,160,92,176,108,256,252,272,2..., dimensions={0} | all-to-all | bytes 131072 | tf_op jit(solution)/shard_map/all_to_all | solution.py:182
  87.1 0.6 unpack.1
Async XLA Ops:
  46.0 11.8 %collective-permute-start.1 = (bf16[256,1152]{1,0:T(8,128)(2,1)S(1)}, bf16[256,1152]{1,0:T(8,128)(2,1)S(1)}, u32[]{:S(2)}, u32[]{:S(2)}) collective-permute-start(bf16[256,1152]{1,0:T(8,128)(2,1)S(1)} %reshape.20.queries_ref), channel_id=1, source_target_pairs={{8,0},{452,508},{24,16},{468,460},{40,32},{484,476},{56,48},{500,4... | collective-permute-start | bytes 1769480 | tf_op jit(solution)/shard_map/ppermute | solution.py:172
  49.0 11.8 %collective-permute-start = (bf16[256,1152]{1,0:T(8,128)(2,1)S(1)}, bf16[256,1152]{1,0:T(8,128)(2,1)S(1)}, u32[]{:S(2)}, u32[]{:S(2)}) collective-permute-start(bf16[256,1152]{1,0:T(8,128)(2,1)S(1)} %reshape.20.queries_ref), channel_id=1, source_target_pairs={{0,8},{508,452},{16,24},{460,468},{32,40},{476,484},{48,56},{492,5... | collective-permute-start | bytes 1769480 | tf_op jit(solution)/shard_map/ppermute | solution.py:171
  61.2 5.6 %collective-permute-start.2 = (f32[8,256]{1,0:T(8,128)S(1)}, f32[8,256]{1,0:T(8,128)S(1)}, u32[]{:S(2)}, u32[]{:S(2)}) collective-permute-start(f32[8,256]{1,0:T(8,128)S(1)} %across.1), channel_id=1, source_target_pairs={{8,0},{452,508},{24,16},{468,460},{40,32},{484,476},{56,48},{500,4... | collective-permute-start | bytes 24584 | tf_op jit(solution)/shard_map/ppermute | solution.py:174

commit v6 on v5

--- a/solution.py
+++ b/solution.py
@@ -77,24 +77,18 @@
     return jnp.max(jnp.where(allowed, scores, -1.0), axis=0, keepdims=True)
 
 
-def across_kernel(before_ref, after_ref, best_ref):
-    width = before_ref.shape[1] - LANES
-    code, last = query_codes(before_ref, width)
-    best = best_of(after_ref, before_ref, code, last, width)
-    best_ref[...] = jnp.broadcast_to(best, best_ref.shape)
-
-
-def own_kernel(queries_ref, before_ref, after_ref, best_ref):
+def near_kernel(queries_ref, before_ref, after_ref, best_ref):
     width = queries_ref.shape[1] - LANES
     code, last = query_codes(queries_ref, width)
     best = best_of(queries_ref, queries_ref, code, last, width)
     best = jnp.maximum(best, best_of(before_ref, queries_ref, code, last, width))
-    best = jnp.maximum(best, best_of(after_ref, queries_ref, code, last, width))
-    best_ref[...] = jnp.broadcast_to(best, best_ref.shape)
+    best_ref[...] = jnp.maximum(best, best_of(after_ref, queries_ref, code, last, width))
 
 
-def spread_kernel(own_ref, across_ref, out_ref):
-    best = jnp.maximum(own_ref[:1, :], across_ref[:1, :])
+def far_kernel(queries_ref, across_ref, best_ref, out_ref):
+    width = queries_ref.shape[1] - LANES
+    code, last = query_codes(queries_ref, width)
+    best = jnp.maximum(best_ref[...], best_of(across_ref, queries_ref, code, last, width))
     messages = out_ref.shape[0]
     count = best.shape[1]
     best = jnp.broadcast_to(best, (messages, count))
@@ -133,15 +127,15 @@
     groups = [[table[member, owner] for owner in range(owners)] for member in range(4)]
     ahead = [(table[m, o], table[(m + 1) % 4, o]) for m in range(4) for o in range(owners)]
     behind = [(b, a) for a, b in ahead]
-    return owners, groups, ahead, behind
+    opposite = [(table[m, o], table[(m + 2) % 4, o]) for m in range(4) for o in range(owners)]
+    return owners, groups, ahead, behind, opposite
 
 
 def make_per_device(docs_axis, split_axis):
     side = round((docs_axis // 2) ** 0.5)
-    owners, groups, ahead, behind = layout(side, side, split_axis)
+    owners, groups, ahead, behind, opposite = layout(side, side, split_axis)
     slots = owners * SLOTS
     both = ("docs", "split")
-    row = jax.ShapeDtypeStruct((8, slots), jnp.float32)
 
     def per_device(embeddings, cluster_id, rank):
         docs, width = embeddings.shape
@@ -170,15 +164,19 @@
         queries = got.reshape(slots, wide)
         before = lax.ppermute(queries, both, ahead)
         after = lax.ppermute(queries, both, behind)
-        across = pl.pallas_call(across_kernel, out_shape=row, compiler_params=SMALL, name="across")(before, after)
-        across = lax.ppermute(across, both, behind)
-        own = pl.pallas_call(own_kernel, out_shape=row, compiler_params=SMALL, name="own")(queries, before, after)
+        across = lax.ppermute(queries, both, opposite)
+        best = pl.pallas_call(
+            near_kernel,
+            out_shape=jax.ShapeDtypeStruct((1, slots), jnp.float32),
+            compiler_params=SMALL,
+            name="near",
+        )(queries, before, after)
         scores = pl.pallas_call(
-            spread_kernel,
+            far_kernel,
             out_shape=jax.ShapeDtypeStruct((owners, LANES), jnp.float32),
             compiler_params=SMALL,
-            name="spread",
-        )(own, across)
+            name="far",
+        )(queries, across, best)
         back = lax.all_to_all(
             scores.reshape(owners, 1, LANES), both, 0, 0, axis_index_groups=groups, tiled=True
         )

time: 88 us -> 89.1 us (1.012)
  the two profiles are of different devices: /device:TPU:1 before, /device:TPU:8 now
where the time goes in v6:
time: 89.1 us; the launch traced here: 88.8 us
  blocking collectives  65.6 us (74%)
  waiting for transfers between devices  11.5 us (13%)
  starting transfers between devices  8.01 us (9%)
  Pallas kernels  3.4 us (4%)
    all_to_all x1, blocking collectives, per_device(): got = lax.all_to_all(send, both, 0, 0, axis_index_groups=groups, tiled=True)  43.5 us
    all_to_all x1, blocking collectives, per_device(): lax.all_to_all(scores.reshape(owners, 1, LANES), both, 0, 0, axis_index_g...  22.2 us
    ppermute x1, waiting for transfers between devices, per_device(): across = lax.ppermute(queries, both, opposite)  5.84 us
    ppermute x1, starting transfers between devices, per_device(): before = lax.ppermute(queries, both, ahead)  3.92 us
    ppermute x1, waiting for transfers between devices, per_device(): after = lax.ppermute(queries, both, behind)  3.75 us
    ppermute x1, starting transfers between devices, per_device(): across = lax.ppermute(queries, both, opposite)  2.16 us
    ppermute x1, waiting for transfers between devices, per_device(): before = lax.ppermute(queries, both, ahead)  1.93 us
    ppermute x1, starting transfers between devices, per_device(): after = lax.ppermute(queries, both, behind)  1.92 us
  transfers between devices with their start and end apart: 3, of which 3 were waited for; matrix products, arithmetic and copies ran while one was open for 0% of the time, Pallas kernels for 1%

profile of v6, /device:TPU:8, one launch (start us, length us, event | category | flops | bytes accessed | tf_op | source)
XLA Modules:
  0.0 88.8 jit_solution(7908982782974381382)
XLA Ops:
  0.0 1.6 %pack.1 = (bf16[128,2,1152]{2,1,0:T(2,128)(2,1)S(1)}, s32[1,128]{1,0:T(1,128)S(1)}) custom-call(bf16[128,1024]{1,0:T(8,128)(2,1)} %rows_hbm.1, s32[1,128]{1,0:T(1,128)} %bitcast.9, s32[1,128]{1,0:T(1,128)} %bitcast.10), custom_call_target="tpu_custom_call" | custom-call | tf_op jit(solution)/shard_map/pack/pallas_call | solution.py:143
  1.6 43.5 %all_to_all.10 = bf16[128,2,1152]{2,1,0:T(2,128)(2,1)S(1)} all-to-all(bf16[128,2,1152]{2,1,0:T(2,128)(2,1)S(1)} %get-tuple-element.7), channel_id=1, replica_groups={{0,508,16,460,32,476,48,492,128,124,144,76,160,92,176,108,256,252,272,2..., dimensions={0} | all-to-all | bytes 1179648 | tf_op jit(solution)/shard_map/all_to_all | solution.py:163
  45.1 0.2 reshape.20.queries_ref
  45.3 1.9 %collective-permute-start.2 = (bf16[256,1152]{1,0:T(8,128)(2,1)S(1)}, bf16[256,1152]{1,0:T(8,128)(2,1)S(1)}, u32[]{:S(2)}, u32[]{:S(2)}) collective-permute-start(bf16[256,1152]{1,0:T(8,128)(2,1)S(1)} %reshape.20.queries_ref), channel_id=1, source_target_pairs={{8,0},{452,508},{24,16},{468,460},{40,32},{484,476},{56,48},{500,4... | collective-permute-start | bytes 1769480 | tf_op jit(solution)/shard_map/ppermute | solution.py:166
  47.2 3.9 %collective-permute-start.1 = (bf16[256,1152]{1,0:T(8,128)(2,1)S(1)}, bf16[256,1152]{1,0:T(8,128)(2,1)S(1)}, u32[]{:S(2)}, u32[]{:S(2)}) collective-permute-start(bf16[256,1152]{1,0:T(8,128)(2,1)S(1)} %reshape.20.queries_ref), channel_id=1, source_target_pairs={{0,8},{508,452},{16,24},{460,468},{32,40},{476,484},{48,56},{492,5... | collective-permute-start | bytes 1769480 | tf_op jit(solution)/shard_map/ppermute | solution.py:165
  51.2 2.2 %collective-permute-start = (bf16[256,1152]{1,0:T(8,128)(2,1)S(1)}, bf16[256,1152]{1,0:T(8,128)(2,1)S(1)}, u32[]{:S(2)}, u32[]{:S(2)}) collective-permute-start(bf16[256,1152]{1,0:T(8,128)(2,1)S(1)} %reshape.20.queries_ref), channel_id=1, source_target_pairs={{0,72},{508,4},{16,88},{460,20},{32,104},{476,36},{48,120},{492,52... | collective-permute-start | bytes 1769480 | tf_op jit(solution)/shard_map/ppermute | solution.py:167
  53.3 3.7 %collective-permute-done.2.after_ref = bf16[256,1152]{1,0:T(8,128)(2,1)S(1)} collective-permute-done((bf16[256,1152]{1,0:T(8,128)(2,1)S(1)}, bf16[256,1152]{1,0:T(8,128)(2,1)S(1)}, u32[]{:S(2)}, u32[]{:S(2)}) %collective-permute-start.2) | collective-permute-done | bytes 589856 | tf_op jit(solution)/shard_map/ppermute | solution.py:166
  57.1 1.9 %collective-permute-done.1.before_ref = bf16[256,1152]{1,0:T(8,128)(2,1)S(1)} collective-permute-done((bf16[256,1152]{1,0:T(8,128)(2,1)S(1)}, bf16[256,1152]{1,0:T(8,128)(2,1)S(1)}, u32[]{:S(2)}, u32[]{:S(2)}) %collective-permute-start.1) | collective-permute-done | bytes 589856 | tf_op jit(solution)/shard_map/ppermute | solution.py:165
  59.0 0.7 near.1.best_ref
  59.7 5.8 %collective-permute-done.across_ref = bf16[256,1152]{1,0:T(8,128)(2,1)S(1)} collective-permute-done((bf16[256,1152]{1,0:T(8,128)(2,1)S(1)}, bf16[256,1152]{1,0:T(8,128)(2,1)S(1)}, u32[]{:S(2)}, u32[]{:S(2)}) %collective-permute-start) | collective-permute-done | bytes 589856 | tf_op jit(solution)/shard_map/ppermute | solution.py:167
  65.6 0.5 far.1
  66.1 22.2 %all_to_all.11 = f32[128,1,128]{2,1,0:T(1,128)S(1)} all-to-all(f32[128,1,128]{2,1,0:T(1,128)S(1)} %bitcast.7), channel_id=1, replica_groups={{0,508,16,460,32,476,48,492,128,124,144,76,160,92,176,108,256,252,272,2..., dimensions={0} | all-to-all | bytes 131072 | tf_op jit(solution)/shard_map/all_to_all | solution.py:180
  88.2 0.6 unpack.1
Async XLA Ops:
  45.3 11.8 %collective-permute-start.2 = (bf16[256,1152]{1,0:T(8,128)(2,1)S(1)}, bf16[256,1152]{1,0:T(8,128)(2,1)S(1)}, u32[]{:S(2)}, u32[]{:S(2)}) collective-permute-start(bf16[256,1152]{1,0:T(8,128)(2,1)S(1)} %reshape.20.queries_ref), channel_id=1, source_target_pairs={{8,0},{452,508},{24,16},{468,460},{40,32},{484,476},{56,48},{500,4... | collective-permute-start | bytes 1769480 | tf_op jit(solution)/shard_map/ppermute | solution.py:166
  47.2 11.8 %collective-permute-start.1 = (bf16[256,1152]{1,0:T(8,128)(2,1)S(1)}, bf16[256,1152]{1,0:T(8,128)(2,1)S(1)}, u32[]{:S(2)}, u32[]{:S(2)}) collective-permute-start(bf16[256,1152]{1,0:T(8,128)(2,1)S(1)} %reshape.20.queries_ref), channel_id=1, source_target_pairs={{0,8},{508,452},{16,24},{460,468},{32,40},{476,484},{48,56},{492,5... | collective-permute-start | bytes 1769480 | tf_op jit(solution)/shard_map/ppermute | solution.py:165
  51.2 14.4 %collective-permute-start = (bf16[256,1152]{1,0:T(8,128)(2,1)S(1)}, bf16[256,1152]{1,0:T(8,128)(2,1)S(1)}, u32[]{:S(2)}, u32[]{:S(2)}) collective-permute-start(bf16[256,1152]{1,0:T(8,128)(2,1)S(1)} %reshape.20.queries_ref), channel_id=1, source_target_pairs={{0,72},{508,4},{16,88},{460,20},{32,104},{476,36},{48,120},{492,52... | collective-permute-start | bytes 1769480 | tf_op jit(solution)/shard_map/ppermute | solution.py:167

commit v7 on v4

--- a/solution.py
+++ b/solution.py
@@ -55,21 +55,20 @@
     return jnp.where(place == 0, 256.0, jnp.where(place == 1, 1.0, 0.0)).astype(jnp.bfloat16)
 
 
-def best_of(keys_ref, queries_ref, width):
+def best_of(keys, queries_ref, width):
     contract = (((1,), (1,)), ((), ()))
-    key_age = jnp.dot(keys_ref[:, width:], age_weights((LANES, LANES), 0), preferred_element_type=jnp.float32)
+    key_age = jnp.dot(keys[:, width:], age_weights((LANES, LANES), 0), preferred_element_type=jnp.float32)
     query_age = lax.dot_general(
         age_weights((8, LANES), 1), queries_ref[:, width:], contract, preferred_element_type=jnp.float32
     )
-    scores = lax.dot_general(
-        keys_ref[:, :width], queries_ref[:, :width], contract, preferred_element_type=jnp.float32
-    )
+    scores = lax.dot_general(keys[:, :width], queries_ref[:, :width], contract, preferred_element_type=jnp.float32)
     allowed = key_age[:, :1] > query_age[:1, :]
     return jnp.max(jnp.where(allowed, scores, -1.0), axis=0, keepdims=True)
 
 
 def make_own(width):
-    def kernel(queries_ref, best_ref):
+    def kernel(got_ref, queries_ref, best_ref):
+        queries_ref[...] = got_ref[...].reshape(queries_ref.shape)
         best_ref[...] = best_of(queries_ref, queries_ref, width)
 
     return kernel
@@ -77,7 +76,7 @@
 
 def make_peer(width):
     def kernel(queries_ref, keys_ref, best_ref, out_ref):
-        best = jnp.maximum(best_ref[...], best_of(keys_ref, queries_ref, width))
+        best = jnp.maximum(best_ref[...], best_of(keys_ref[...].reshape(queries_ref.shape), queries_ref, width))
         messages = out_ref.shape[0]
         count = best.shape[1]
         best = jnp.broadcast_to(best, (messages, count))
@@ -135,14 +134,17 @@
             pltpu.with_memory_space_constraint(cluster_id.reshape(1, docs), pltpu.HBM),
             pltpu.with_memory_space_constraint(rank.reshape(1, docs), pltpu.HBM),
         )
-        got = lax.all_to_all(
-            send, both, 0, 0, axis_index_groups=groups, tiled=True
-        )
-        queries = got.reshape(slots, wide)
-        keys = lax.ppermute(queries, "docs", partner)
-        best = pl.pallas_call(
-            make_own(width), out_shape=jax.ShapeDtypeStruct((1, slots), jnp.float32), name="own", compiler_params=PARAMS
-        )(queries)
+        got = lax.all_to_all(send, both, 0, 0, axis_index_groups=groups, tiled=True)
+        keys = lax.ppermute(got, "docs", partner)
+        queries, best = pl.pallas_call(
+            make_own(width),
+            out_shape=(
+                jax.ShapeDtypeStruct((slots, wide), jnp.bfloat16),
+                jax.ShapeDtypeStruct((1, slots), jnp.float32),
+            ),
+            name="own",
+            compiler_params=PARAMS,
+        )(got)
         scores = pl.pallas_call(
             make_peer(width),
             out_shape=jax.ShapeDtypeStruct((clusters, LANES), jnp.float32),

time: 87.3 us -> 86.9 us (level)
  no operation moved by 1% of the time
where the time goes in v7:
time: 86.9 us; the launch traced here: 86.7 us
  blocking collectives  75.7 us (87%)
  starting transfers between devices  5.02 us (6%)
  Pallas kernels  4.37 us (5%)
  waiting for transfers between devices  1.53 us (2%)
    all_to_all x1, blocking collectives, per_device(): got = lax.all_to_all(send, both, 0, 0, axis_index_groups=groups, tiled=True)  54.1 us
    all_to_all x1, blocking collectives, per_device(): lax.all_to_all(scores.reshape(clusters, 1, LANES), both, 0, 0, axis_index...  21.6 us
    ppermute x1, starting transfers between devices, per_device(): keys = lax.ppermute(got, 'docs', partner)  5.02 us
    pallas_call x1, Pallas kernels, per_device(): pl.pallas_call(pack_kernel, out_shape=(jax.ShapeDtypeStruct((clusters, SL...  1.76 us
  transfers between devices with their start and end apart: 1, of which 1 were waited for; matrix products, arithmetic and copies ran while one was open for 0% of the time, Pallas kernels for 1%

profile of v7, /device:TPU:1, one launch (start us, length us, event | category | flops | bytes accessed | tf_op | source)
XLA Modules:
  0.0 86.7 jit_solution(8947945979057620401)
XLA Ops:
  0.0 1.8 %pack.1 = (bf16[256,2,1152]{2,1,0:T(2,128)(2,1)S(1)}, s32[1,128]{1,0:T(1,128)S(1)}) custom-call(bf16[128,1024]{1,0:T(8,128)(2,1)} %rows_hbm.1, s32[1,128]{1,0:T(1,128)} %bitcast.9, s32[1,128]{1,0:T(1,128)} %bitcast.10), custom_call_target="tpu_custom_call" | custom-call | tf_op jit(solution)/shard_map/pack/pallas_call | solution.py:118
  1.8 54.1 %all_to_all.10.got_ref = bf16[256,2,1152]{2,1,0:T(2,128)(2,1)S(1)} all-to-all(bf16[256,2,1152]{2,1,0:T(2,128)(2,1)S(1)} %get-tuple-element.9), channel_id=1, replica_groups={{0,1,2,3,8,9,10,11,16,17,18,19,24,25,26,27,32,33,34,35,40,41,42,43,48,4..., dimensions={0} | all-to-all | bytes 2359296 | tf_op jit(solution)/shard_map/all_to_all | solution.py:137
  55.9 5.0 %collective-permute-start = (bf16[256,2,1152]{2,1,0:T(2,128)(2,1)S(1)}, bf16[256,2,1152]{2,1,0:T(2,128)(2,1)S(1)}, u32[]{:S(2)}, u32[]{:S(2)}) collective-permute-start(bf16[256,2,1152]{2,1,0:T(2,128)(2,1)S(1)} %all_to_all.10.got_ref), channel_id=1, source_target_pairs={{0,4},{4,0},{8,12},{12,8},{16,20},{20,16},{24,28},{28,24},{32,36},... | collective-permute-start | bytes 3538952 | tf_op jit(solution)/shard_map/ppermute | solution.py:138
  60.9 0.9 %own.1 = (bf16[512,1152]{1,0:T(8,128)(2,1)S(1)}, f32[1,512]{1,0:T(1,128)S(1)}) custom-call(bf16[256,2,1152]{2,1,0:T(2,128)(2,1)S(1)} %all_to_all.10.got_ref), custom_call_target="tpu_custom_call" | custom-call | tf_op jit(solution)/shard_map/own/pallas_call | solution.py:139
  61.8 1.5 %collective-permute-done.keys_ref = bf16[256,2,1152]{2,1,0:T(2,128)(2,1)S(1)} collective-permute-done((bf16[256,2,1152]{2,1,0:T(2,128)(2,1)S(1)}, bf16[256,2,1152]{2,1,0:T(2,128)(2,1)S(1)}, u32[]{:S(2)}, u32[]{:S(2)}) %collective-permute-start) | collective-permute-done | bytes 1179680 | tf_op jit(solution)/shard_map/ppermute | solution.py:138
  63.3 1.0 %peer.1 = f32[256,128]{1,0:T(8,128)S(1)} custom-call(bf16[512,1152]{1,0:T(8,128)(2,1)S(1)} %get-tuple-element.10.queries_ref, bf16[256,2,1152]{2,1,0:T(2,128)(2,1)S(1)} %collective-permute-done.keys_ref, f32[1,512]{1,0:T(1,128)S(1)} %get-tuple-element.11.best_ref), custom_call_target="tpu_custom_call" | custom-call | tf_op jit(solution)/shard_map/peer/pallas_call | solution.py:148
  64.4 21.6 %all_to_all.11 = f32[256,1,128]{2,1,0:T(1,128)S(1)} all-to-all(f32[256,1,128]{2,1,0:T(1,128)S(1)} %bitcast.7), channel_id=1, replica_groups={{0,1,2,3,8,9,10,11,16,17,18,19,24,25,26,27,32,33,34,35,40,41,42,43,48,4..., dimensions={0} | all-to-all | bytes 262144 | tf_op jit(solution)/shard_map/all_to_all | solution.py:153
  86.0 0.7 unpack.1
Async XLA Ops:
  55.9 7.5 %collective-permute-start = (bf16[256,2,1152]{2,1,0:T(2,128)(2,1)S(1)}, bf16[256,2,1152]{2,1,0:T(2,128)(2,1)S(1)}, u32[]{:S(2)}, u32[]{:S(2)}) collective-permute-start(bf16[256,2,1152]{2,1,0:T(2,128)(2,1)S(1)} %all_to_all.10.got_ref), channel_id=1, source_target_pairs={{0,4},{4,0},{8,12},{12,8},{16,20},{20,16},{24,28},{28,24},{32,36},... | collective-permute-start | bytes 3538952 | tf_op jit(solution)/shard_map/ppermute | solution.py:138
